TPU v7x, 512 devices: a whole 4x4x16 slice. The times are simulated.
512 devices in a mesh: pole: 8 (over z_hi, y), space: 64 (over z_lo, x, core).
Axes of the slice: x: 4, y: 4, z: 16 (z_hi: 2, z_lo: 8; z = z_hi * 8 + z_lo), core: 2. Of those that a mesh axis runs over, the one named last changes fastest.
Arguments:
- conductivity: float32 [128, 64, 128], P('space'), may hold values from 0.1 to 10
- misfit: float32 [128, 64, 128], P('space'), may hold values from -6 to 6
- forward_states: float32 [16, 128, 64, 128], P('pole', 'space'), may hold values from -6 to 6
- pole_shifts: float32 [16], replicated, may hold values from 0.01 to 10
- pole_weights: float32 [16], replicated, may hold values from 0.05 to 1
- pole_order: int32 [16], P('pole'), may hold values from 0 to 15, each once
Outputs:
- adjoint_states: float32 [16, 128, 64, 128], P('pole', 'space')
- gradient: float32 [128, 64, 128], P('space', 'pole')
Inputs may be any that keep to these rules, and one draw needn't show every extreme that they name: `pole_order`: every pole stands in exactly one slot.
All inputs are finite; a program needn't handle non-finite values.
Results may differ from a plain program's by a relative error of at most 0.0001.
Values sent between devices are 32-bit elements; how exact they have to be, the bound alone decides.
A program may use at most 128 MiB of HBM per device.

v0:
```python
import jax
import jax.numpy as jnp
from jax import lax
from jax.sharding import PartitionSpec as P

ITERS = 2


DAMPING = 0.8


def extended(array, sides, width):
    for axis, dim in sides:
        peers, length = (lax.axis_size(axis), array.shape[dim])
        up = [(i, (i + 1) % peers) for i in range(peers - 1)]
        down = [(j, i) for i, j in up]
        last = lax.slice_in_dim(array, length - width, length, axis=dim)
        leading = lax.slice_in_dim(array, 0, width, axis=dim)
        before = lax.ppermute(last, axis, up)
        after = lax.ppermute(leading, axis, down)
        array = jnp.concatenate([before, array, after], axis=dim)
    return array


def plus_side(field, which_dim):
    extent = field.shape[which_dim]
    inner_part = lax.slice_in_dim(field, 1, extent, axis=which_dim)
    zero_plane = jnp.zeros_like(lax.slice_in_dim(field, 0, 1, axis=which_dim))
    return jnp.concatenate([inner_part, zero_plane], axis=which_dim)


def minus_side(field, which_dim):
    extent = field.shape[which_dim]
    inner_part = lax.slice_in_dim(field, 0, extent - 1, axis=which_dim)
    zero_plane = jnp.zeros_like(lax.slice_in_dim(field, 0, 1, axis=which_dim))
    return jnp.concatenate([zero_plane, inner_part], axis=which_dim)


def coarse_pick(faces, which_dim, offset):
    extent_x, extent_y, extent_z = faces.shape
    blocks = faces.reshape(extent_x // 2, 2, extent_y // 2, 2, extent_z // 2, 2)
    chosen = lax.index_in_dim(blocks, offset, axis=2 * which_dim + 1, keepdims=True)
    return jnp.sum(chosen, axis=(1, 3, 5))


def side_terms(field, plus_faces, minus_faces, widened):
    result = plus_faces[0] * (field - widened[:, 2:]) + minus_faces[0] * (field - widened[:, :-2])
    for which_dim in (1, 2):
        result = result + plus_faces[which_dim] * (field - plus_side(field, which_dim + 1))
        result = result + minus_faces[which_dim] * (field - minus_side(field, which_dim + 1))
    return result


def fine_image(field, plus_faces, minus_faces, shift_value):
    widened = extended(field, (("space", 1),), 1)
    return shift_value * field + side_terms(field, plus_faces, minus_faces, widened)


def coarse_image(field, plus_faces, minus_faces, shift_value):
    widened = extended(field, (("space", 1),), 1)
    return shift_value * field + side_terms(field, plus_faces, minus_faces, widened)


def restrict(field):
    members, extent_x, extent_y, extent_z = field.shape
    shaped = field.reshape(members, extent_x // 2, 2, extent_y // 2, 2, extent_z // 2, 2)
    return jnp.sum(shaped, axis=(2, 4, 6))


def prolong(field):
    return jnp.repeat(jnp.repeat(jnp.repeat(field, 2, axis=1), 2, axis=2), 2, axis=3)


def precondition(residual, fine, coarse):
    plus_faces, minus_faces, shift_value, diagonal = fine
    coarse_plus, coarse_minus, coarse_shift, coarse_diagonal = coarse
    smooth_one = DAMPING * residual / diagonal
    coarse_rhs = restrict(residual - fine_image(smooth_one, plus_faces, minus_faces, shift_value))
    coarse_one = DAMPING * coarse_rhs / coarse_diagonal
    coarse_two = (
        coarse_one
        + DAMPING
        * (coarse_rhs - coarse_image(coarse_one, coarse_plus, coarse_minus, coarse_shift))
        / coarse_diagonal
    )
    corrected = smooth_one + prolong(coarse_two)
    return (
        corrected
        + DAMPING
        * (residual - fine_image(corrected, plus_faces, minus_faces, shift_value))
        / diagonal
    )


def expand(values):
    return values.reshape(-1, 1, 1, 1)


def cell_sums(values):
    return jnp.sum(values, axis=(1, 2, 3))


def norm_sum(residual, precond):
    return lax.psum(cell_sums(residual * precond), "space")


def solve(rhs, fine, coarse):
    plus_faces, minus_faces, shift_value, diagonal = fine
    iterate = jnp.zeros_like(rhs)
    residual = rhs
    precond = precondition(residual, fine, coarse)
    gamma_now = norm_sum(residual, precond)
    search = precond
    for turn_index in range(ITERS):
        image_field = fine_image(search, plus_faces, minus_faces, shift_value)
        curve = lax.psum(cell_sums(search * image_field), "space")
        step_length = gamma_now / curve
        iterate = iterate + expand(step_length) * search
        if turn_index + 1 < ITERS:
            residual = residual - expand(step_length) * image_field
            precond = precondition(residual, fine, coarse)
            gamma_next = norm_sum(residual, precond)
            search = precond + expand(gamma_next / gamma_now) * search
            gamma_now = gamma_next
    return iterate


def per_device(conductivity, misfit, forward_states, pole_shifts, pole_weights, pole_order):
    widened_kappa = extended(conductivity, (("space", 0),), 1)
    plus_faces = [
        0.5 * (conductivity + widened_kappa[2:]),
        0.5 * (conductivity + plus_side(conductivity, 1)),
        0.5 * (conductivity + plus_side(conductivity, 2)),
    ]
    minus_faces = [
        0.5 * (conductivity + widened_kappa[:-2]),
        0.5 * (conductivity + minus_side(conductivity, 1)),
        0.5 * (conductivity + minus_side(conductivity, 2)),
    ]
    base_diagonal = (
        plus_faces[0]
        + plus_faces[1]
        + plus_faces[2]
        + minus_faces[0]
        + minus_faces[1]
        + minus_faces[2]
    )
    coarse_plus = [coarse_pick(plus_faces[which_dim], which_dim, 1) for which_dim in range(3)]
    coarse_minus = [coarse_pick(minus_faces[which_dim], which_dim, 0) for which_dim in range(3)]
    coarse_base = (
        coarse_plus[0]
        + coarse_plus[1]
        + coarse_plus[2]
        + coarse_minus[0]
        + coarse_minus[1]
        + coarse_minus[2]
    )
    pole_index = jnp.arange(pole_shifts.shape[0], dtype=jnp.int32)
    matches = pole_order[:, None] == pole_index[None, :]
    shift_local = jnp.sum(jnp.where(matches, pole_shifts[None, :], 0.0), axis=1)
    weight_local = jnp.sum(jnp.where(matches, pole_weights[None, :], 0.0), axis=1)
    members = forward_states.shape[0]

    def solve_group(shift_part, weight_part):
        shift_value = expand(shift_part)
        fine = (plus_faces, minus_faces, shift_value, base_diagonal[None] + shift_value)
        coarse = (
            coarse_plus,
            coarse_minus,
            8.0 * shift_value,
            coarse_base[None] + 8.0 * shift_value,
        )
        return solve(expand(weight_part) * misfit[None], fine, coarse)

    adjoint_states = jnp.concatenate(
        [
            solve_group(shift_local[member : member + 1], weight_local[member : member + 1])
            for member in range(members)
        ],
        axis=0,
    )
    widened = extended(jnp.stack([adjoint_states, forward_states]), (("space", 2),), 1)
    term = (adjoint_states - widened[0, :, 2:]) * (forward_states - widened[1, :, 2:])
    term = term + (adjoint_states - widened[0, :, :-2]) * (forward_states - widened[1, :, :-2])
    for which_dim in (2, 3):
        term = term + (adjoint_states - plus_side(adjoint_states, which_dim)) * (
            forward_states - plus_side(forward_states, which_dim)
        )
        term = term + (adjoint_states - minus_side(adjoint_states, which_dim)) * (
            forward_states - minus_side(forward_states, which_dim)
        )
    local_term = -0.5 * jnp.sum(term, axis=0)
    gradient = lax.psum_scatter(local_term, "pole", scatter_dimension=1, tiled=True)
    return (adjoint_states, gradient)


def solution(mesh):
    in_specs = (
        P("space", None, None),
        P("space", None, None),
        P("pole", "space", None, None),
        P(),
        P(),
        P("pole"),
    )
    out_specs = (P("pole", "space", None, None), P("space", "pole", None))
    return jax.shard_map(
        per_device, mesh=mesh, in_specs=in_specs, out_specs=out_specs, check_vma=False
    )
```

profile of v0, /device:TPU:1, one launch (start us, length us, event | category | flops | bytes accessed | tf_op | source)
XLA Modules:
  0.0 1186.1 jit_solution(15605405225843215051)
XLA Ops:
  8.0 8.8 collective-permute-start
  16.8 1.9 collective-permute-start.1
  26.1 2.3 fusion.175
  28.5 2.1 fusion.173
  31.3 2.4 collective-permute-start.2
  33.7 3.2 collective-permute-start.3
  36.8 5.5 reshape.590
  42.4 2.5 slice_reduce_fusion
  44.9 5.5 reshape.587
  50.4 3.6 slice_reduce_fusion.1
  54.1 5.5 reshape.589
  59.6 1.9 slice_reduce_fusion.2
  61.6 5.5 reshape.588
  67.1 1.9 slice_reduce_fusion.3
  69.0 5.5 reshape.586
  74.5 2.0 slice_reduce_fusion.4
  76.5 5.5 reshape.585
  82.0 1.9 slice_reduce_fusion.5
  84.0 1.9 collective-permute-start.18
  85.9 3.8 collective-permute-start.19
  91.2 2.1 reduce_sum.256
  94.3 1.9 collective-permute-start.4
  96.2 3.6 collective-permute-start.5
  99.9 2.1 fusion.89
  102.0 2.1 reduce_sum.284
  105.3 1.9 collective-permute-start.20
  107.3 3.6 collective-permute-start.21
  112.0 2.6 add_bitcast_fusion
  114.8 1.9 collective-permute-start.6
  116.7 4.2 collective-permute-start.7
  121.0 1.9 collective-permute-start.22
  122.9 3.6 collective-permute-start.23
  130.8 1.9 collective-permute-start.8
  132.7 3.7 collective-permute-start.9
  137.0 1.9 collective-permute-start.24
  138.9 3.6 collective-permute-start.25
  142.6 2.0 multiply_reduce_fusion.3
  144.6 212.7 %all-reduce.79 = (f32[1]{0:T(128)}, f32[1]{0:T(128)}) all-reduce(f32[1]{0:T(128)} %bitcast.25, f32[1]{0:T(128)} %bitcast.26), channel_id=1, replica_groups=mesh['pole'=8,'space'=64] {'space'}, use_global_device_ids=true, to_apply=%region_11.12 | all-reduce | flops 2 | bytes 16 | tf_op jit(solution)/shard_map/psum | solution.py:104
  360.0 9.7 collective-permute-start.10
  369.7 1.9 collective-permute-start.11
  374.2 2.1 reduce_sum.276
  376.7 2.1 collective-permute-start.12
  378.8 3.9 collective-permute-start.13
  385.2 1.9 collective-permute-start.14
  387.1 4.2 collective-permute-start.15
  392.3 4.3 multiply_reduce_fusion.2
  396.6 208.2 %all-reduce.78 = (f32[1]{0:T(128)}, f32[1]{0:T(128)}) all-reduce(f32[1]{0:T(128)} %bitcast.49, f32[1]{0:T(128)} %bitcast.50), channel_id=1, replica_groups=mesh['pole'=8,'space'=64] {'space'}, use_global_device_ids=true, to_apply=%region_23.24 | all-reduce | flops 2 | bytes 16 | tf_op jit(solution)/shard_map/psum | solution.py:104
  607.3 5.0 collective-permute-start.26
  612.3 1.9 collective-permute-start.27
  616.7 2.1 reduce_sum.292
  619.2 2.2 collective-permute-start.28
  621.4 3.9 collective-permute-start.29
  627.8 1.9 collective-permute-start.30
  629.7 4.2 collective-permute-start.31
  634.9 1.9 multiply_reduce_fusion
  636.8 208.3 %all-reduce.77 = (f32[1]{0:T(128)}, f32[1]{0:T(128)}) all-reduce(f32[1]{0:T(128)} %bitcast.56, f32[1]{0:T(128)} %bitcast.32), channel_id=1, replica_groups=mesh['pole'=8,'space'=64] {'space'}, use_global_device_ids=true, to_apply=%region_29.30 | all-reduce | flops 2 | bytes 16 | tf_op jit(solution)/shard_map/psum | solution.py:104
  847.9 5.0 collective-permute-start.16
  853.0 1.9 collective-permute-start.17
  854.9 2.4 collective-permute-start.32
  857.3 3.2 collective-permute-start.33
  863.2 209.5 %all-reduce.76 = (f32[1]{0:T(128)}, f32[1]{0:T(128)}) all-reduce(f32[1]{0:T(128)} %bitcast.58, f32[1]{0:T(128)} %bitcast.34), channel_id=1, replica_groups=mesh['pole'=8,'space'=64] {'space'}, use_global_device_ids=true, to_apply=%region_31.32 | all-reduce | flops 2 | bytes 16 | tf_op jit(solution)/shard_map/psum | solution.py:116
  1075.3 3.8 collective-permute-start.34
  1079.2 1.9 collective-permute-start.35
  1084.5 94.7 %reduce-scatter.2.cloned.1.call-done = f32[2,8,128]{2,1,0:T(8,128)} async-done(((f32[2,64,128]{2,1,0:T(8,128)}), f32[2,8,128]{2,1,0:T(8,128)}) %reduce-scatter.2.cloned.1.call-update) | async-done | bytes 8208 | tf_op jit(solution)/shard_map/reduce_scatter | solution.py:193
  (148 shorter events, 39.1 us)
Async XLA Ops:
  7.2 1172.1 %reduce-scatter.2.cloned.1.call-start = ((), (), s32[]{:S(2)}) async-start(), calls=%async_computation.1 | async-start | bytes 73728 | tf_op jit(solution)/shard_map/reduce_scatter | solution.py:193
  8.0 18.0 %collective-permute-start = (f32[1,64,128]{2,1,0:T(8,128)S(1)}, f32[1,64,128]{2,1,0:T(8,128)S(1)}, u32[]{:S(2)}, u32[]{:S(2)}) collective-permute-start(f32[1,64,128]{2,1,0:T(8,128)S(1)} %get-tuple-element.121), channel_id=1, source_target_pairs={{1,0},{2,1},{3,2},{4,3},{5,4},{6,5},{7,6},{8,7},{9,8},{10,9},{11,1... | collective-permute-start | bytes 98312 | tf_op jit(solution)/shard_map/ppermute | solution.py:20
  16.8 9.3 collective-permute-start.1
  31.3 58.5 %collective-permute-start.2 = (f32[1,1,64,128]{3,2,1,0:T(8,128)S(1)}, f32[1,1,64,128]{3,2,1,0:T(8,128)S(1)}, u32[]{:S(2)}, u32[]{:S(2)}) collective-permute-start(f32[1,1,64,128]{3,2,1,0:T(8,128)S(1)} %get-tuple-element.114), channel_id=1, source_target_pairs={{1,0},{2,1},{3,2},{4,3},{5,4},{6,5},{7,6},{8,7},{9,8},{10,9},{11,1... | collective-permute-start | bytes 98312 | tf_op jit(solution)/shard_map/ppermute | solution.py:20
  33.7 56.1 %collective-permute-start.3 = (f32[1,1,64,128]{3,2,1,0:T(8,128)S(1)}, f32[1,1,64,128]{3,2,1,0:T(8,128)S(1)}, u32[]{:S(2)}, u32[]{:S(2)}) collective-permute-start(f32[1,1,64,128]{3,2,1,0:T(8,128)S(1)} %get-tuple-element.115), channel_id=1, source_target_pairs={{0,1},{1,2},{2,3},{3,4},{4,5},{5,6},{6,7},{7,8},{8,9},{9,10},{10,1... | collective-permute-start | bytes 98312 | tf_op jit(solution)/shard_map/ppermute | solution.py:19
  74.5 15.2 %copy-start = (f32[2,64,128]{2,1,0:T(8,128)S(1)}, f32[2,64,128]{2,1,0:T(8,128)}, u32[]{:S(2)}) copy-start(f32[2,64,128]{2,1,0:T(8,128)} %param.7) | copy-start | bytes 196612
  84.0 15.9 %collective-permute-start.18 = (f32[1,1,64,128]{3,2,1,0:T(8,128)}, f32[1,1,64,128]{3,2,1,0:T(8,128)}, u32[]{:S(2)}, u32[]{:S(2)}) collective-permute-start(f32[1,1,64,128]{3,2,1,0:T(8,128)} %get-tuple-element.96), channel_id=1, source_target_pairs={{1,0},{2,1},{3,2},{4,3},{5,4},{6,5},{7,6},{8,7},{9,8},{10,9},{11,1... | collective-permute-start | bytes 98312 | tf_op jit(solution)/shard_map/ppermute | solution.py:20
  85.9 14.0 %collective-permute-start.19 = (f32[1,1,64,128]{3,2,1,0:T(8,128)}, f32[1,1,64,128]{3,2,1,0:T(8,128)}, u32[]{:S(2)}, u32[]{:S(2)}) collective-permute-start(f32[1,1,64,128]{3,2,1,0:T(8,128)} %get-tuple-element.97), channel_id=1, source_target_pairs={{0,1},{1,2},{2,3},{3,4},{4,5},{5,6},{6,7},{7,8},{8,9},{9,10},{10,1... | collective-permute-start | bytes 98312 | tf_op jit(solution)/shard_map/ppermute | solution.py:19
  94.3 10.1 collective-permute-start.4
  96.2 8.2 collective-permute-start.5
  102.0 2.5 copy-start.3
  102.0 2.5 copy-start.4
  105.3 5.9 collective-permute-start.20
  107.3 4.5 collective-permute-start.21
  114.8 11.7 collective-permute-start.6
  116.7 9.8 collective-permute-start.7
  121.0 7.1 collective-permute-start.22
  122.9 5.2 collective-permute-start.23
  130.8 11.8 collective-permute-start.8
  132.7 9.9 collective-permute-start.9
  137.0 254.4 %collective-permute-start.24 = (f32[1,1,64,128]{3,2,1,0:T(8,128)}, f32[1,1,64,128]{3,2,1,0:T(8,128)}, u32[]{:S(2)}, u32[]{:S(2)}) collective-permute-start(f32[1,1,64,128]{3,2,1,0:T(8,128)} %get-tuple-element.68), channel_id=1, source_target_pairs={{1,0},{2,1},{3,2},{4,3},{5,4},{6,5},{7,6},{8,7},{9,8},{10,9},{11,1... | collective-permute-start | bytes 98312 | tf_op jit(solution)/shard_map/ppermute | solution.py:20
  138.9 252.5 %collective-permute-start.25 = (f32[1,1,64,128]{3,2,1,0:T(8,128)}, f32[1,1,64,128]{3,2,1,0:T(8,128)}, u32[]{:S(2)}, u32[]{:S(2)}) collective-permute-start(f32[1,1,64,128]{3,2,1,0:T(8,128)} %get-tuple-element.69), channel_id=1, source_target_pairs={{0,1},{1,2},{2,3},{3,4},{4,5},{5,6},{6,7},{7,8},{8,9},{9,10},{10,1... | collective-permute-start | bytes 98312 | tf_op jit(solution)/shard_map/ppermute | solution.py:19
  360.0 11.7 collective-permute-start.10
  369.7 3.1 collective-permute-start.11
  376.7 6.1 collective-permute-start.12
  378.8 4.8 collective-permute-start.13
  385.2 6.2 collective-permute-start.14
  387.1 5.2 collective-permute-start.15
  607.3 7.0 collective-permute-start.26
  612.3 3.1 collective-permute-start.27
  618.8 456.5 %copy-start.1 = (f32[2,2,64,128]{3,2,1,0:T(8,128)S(1)}, f32[2,2,64,128]{3,2,1,0:T(8,128)}, u32[]{:S(2)}) copy-start(f32[2,2,64,128]{3,2,1,0:T(8,128)} %param.8) | copy-start | bytes 393220
  619.2 463.8 %copy-start.2 = (f32[2,2,64,127]{3,2,1,0:T(8,128)S(1)}, f32[2,2,64,127]{3,2,1,0:T(8,128)}, u32[]{:S(2)}) copy-start(f32[2,2,64,127]{3,2,1,0:T(8,128)} %get-tuple-element.41) | copy-start | bytes 390148
  619.2 6.2 collective-permute-start.28
  621.4 4.8 collective-permute-start.29
  627.8 6.2 collective-permute-start.30
  629.7 5.2 collective-permute-start.31
  847.9 12.5 %collective-permute-start.16 = (f32[1,1,64,128]{3,2,1,0:T(8,128)S(1)}, f32[1,1,64,128]{3,2,1,0:T(8,128)S(1)}, u32[]{:S(2)}, u32[]{:S(2)}) collective-permute-start(f32[1,1,64,128]{3,2,1,0:T(8,128)S(1)} %get-tuple-element.44), channel_id=1, source_target_pairs={{1,0},{2,1},{3,2},{4,3},{5,4},{6,5},{7,6},{8,7},{9,8},{10,9},{11,1... | collective-permute-start | bytes 98312 | tf_op jit(solution)/shard_map/ppermute | solution.py:20
  853.0 7.5 collective-permute-start.17
  854.9 7.0 collective-permute-start.32
  857.3 4.6 collective-permute-start.33
  1075.3 6.3 collective-permute-start.34
  1079.2 3.9 collective-permute-start.35
Sparse Core Ops, SparseCore 0:
  1084.0 95.1 reduce-scatter.1
where the time goes:
time: 1190 us
  blocking collectives  839 us (71%)
  starting transfers between devices  117 us (10%)
  waiting for transfers between devices  103 us (9%)
  local copies, waits for them, and re-layouts  52.8 us (4%)
  other arithmetic  51 us (4%)
  between operations  23.9 us (2%)
    psum x3, blocking collectives, norm_sum(): return lax.psum(cell_sums(residual * precond), 'space')  629 us
    psum x1, blocking collectives, solve(): curve = lax.psum(cell_sums(search * image_field), 'space')  209 us
    reduce_scatter x1, waiting for transfers between devices, per_device(): lax.psum_scatter(local_term, 'pole', scatter_dimension=1, tiled=True)  94.7 us
    ppermute x18, starting transfers between devices, extended(): after = lax.ppermute(leading, axis, down)  58.6 us
    ppermute x18, starting transfers between devices, extended(): before = lax.ppermute(last, axis, up)  58.4 us
    reshape x6, local copies, waits for them, and re-layouts, coarse_pick(): blocks = faces.reshape(extent_x // 2, 2, extent_y // 2, 2, extent_z // 2, 2)  33.1 us
  transfers between devices with their start and end apart: 37, of which 10 were waited for; matrix products, arithmetic and copies ran while one was open for 6% of the time, Pallas kernels for 0%

commit v1 on v0

v1 whole, which is shorter than its diff:
```python
import functools

import jax
import jax.numpy as jnp
from jax import lax
from jax.experimental import pallas as pl
from jax.experimental.pallas import tpu as pltpu
from jax.sharding import PartitionSpec as P

MESH = pl.DeviceIdType.MESH
W = 0.8
NY, NZ = 64, 128
HALO = 12
PLANES = 4 + 2 * HALO


def roll(value, shift, axis):
    return pltpu.roll(value, shift % value.shape[axis], axis)


def pair_sum(value):
    value = value + roll(value, -1, 1)
    return value + roll(value, -1, 0)


def kernel(
    chips, poles,
    shift_ref, weight_ref, order_ref, kappa_ref, misfit_ref, forward_ref,
    adjoint_ref, gradient_ref,
    kap, res, face_x, face_y, face_z, diag, gain, z1, z2, u0, rt, ut,
    cgain, cface_x, cface_y, cface_z, y1,
    fwd, sib_u, sib_t, xout, part, sums, swap, term, pieces, gout,
    near_send, near_recv, sib_send, sib_recv, f_send, f_recv, loc, ar_send, ar_recv, sw_send, sw_recv,
    xs_send, xs_recv, rs_send, rs_recv,
):
    pole = lax.axis_index("pole")
    space = lax.axis_index("space")
    core = lax.rem(space, 2)
    chip = space // 2
    sibling = space + 1 - 2 * core
    steps = (1, -1, 2, -2, 3, -3)

    def has(step):
        return jnp.logical_and(chip + step >= 0, chip + step < chips)

    barrier = pltpu.get_barrier_semaphore()

    def greet(p, s):
        pl.semaphore_signal(barrier, inc=1, device_id=(p, s), device_id_type=MESH)

    def near(p_space):
        return (pole, p_space)

    greet(pole, sibling)

    def greet_chip(d, carry):
        greet(pole, lax.rem(space + 2 * d, 2 * chips))
        return carry

    lax.fori_loop(1, chips, greet_chip, 0)
    for d in range(1, poles):
        greet(lax.rem(pole + d, poles), space)
    across = space + 2 * core - 1
    has_across = jnp.logical_and(across >= 0, across < 2 * chips)

    @pl.when(has_across)
    def _():
        greet(pole, across)

    own = HALO + 2 * core
    own_copies = [
        pltpu.make_async_copy(kappa_ref, kap.at[pl.ds(own, 2)], loc.at[0]),
        pltpu.make_async_copy(misfit_ref, res.at[pl.ds(own, 2)], loc.at[1]),
        pltpu.make_async_copy(forward_ref, fwd.at[:, pl.ds(1, 2)], loc.at[2]),
    ]
    for copy in own_copies:
        copy.start()
    for step in steps:
        @pl.when(jnp.logical_not(has(step)))
        def _():
            zeros = jnp.zeros((4, NY, NZ), jnp.float32)
            kap[pl.ds(HALO + 4 * step, 4)] = zeros
            res[pl.ds(HALO + 4 * step, 4)] = zeros

    @pl.when(space == 0)
    def _():
        fwd[:, 0] = jnp.zeros((2, NY, NZ), jnp.float32)

    @pl.when(space == 2 * chips - 1)
    def _():
        fwd[:, 3] = jnp.zeros((2, NY, NZ), jnp.float32)

    pl.semaphore_wait(barrier, chips + poles - 1 + has_across.astype(jnp.int32))

    def remote(src, dst, send, recv, target):
        return pltpu.make_async_remote_copy(
            src_ref=src, dst_ref=dst, send_sem=send, recv_sem=recv,
            device_id=target, device_id_type=MESH,
        )

    def outgoing(i, step):
        at = own - 4 * step
        return [
            remote(source, dest.at[pl.ds(at, 2)], near_send.at[a, i], near_recv.at[a, i],
                   near(space + 2 * step))
            for a, (source, dest) in enumerate(((kappa_ref, kap), (misfit_ref, res)))
        ]

    def incoming(i, step):
        at = own - 4 * step
        return [
            remote(source, dest.at[pl.ds(at, 2)], near_send.at[a, i], near_recv.at[a, i],
                   near(space - 2 * step))
            for a, (source, dest) in enumerate(((kappa_ref, kap), (misfit_ref, res)))
        ]

    def passing(i, at):
        return [
            remote(dest.at[pl.ds(at, 2)], dest.at[pl.ds(at, 2)], sib_send.at[a, i], sib_recv.at[a, i],
                   near(sibling))
            for a, dest in enumerate((kap, res))
        ]

    def taken(i, at):
        return [
            remote(dest.at[pl.ds(at, 2)], dest.at[pl.ds(at, 2)], sib_send.at[a, i], sib_recv.at[a, i],
                   near(sibling))
            for a, dest in enumerate((kap, res))
        ]

    for i, step in enumerate(steps):
        @pl.when(has(step))
        def _():
            for copy in outgoing(i, step):
                copy.start()

    for copy in own_copies:
        copy.wait()
    for copy in passing(6, own):
        copy.start()

    previous, following = space - 1, space + 1
    to_previous = remote(forward_ref.at[:, 0], fwd.at[:, 3], f_send.at[0], f_recv.at[0], near(previous))
    to_following = remote(forward_ref.at[:, 1], fwd.at[:, 0], f_send.at[1], f_recv.at[1], near(following))

    @pl.when(space > 0)
    def _():
        to_previous.start()

    @pl.when(space < 2 * chips - 1)
    def _():
        to_following.start()

    for i, step in enumerate(steps):
        @pl.when(has(-step))
        def _():
            for copy in incoming(i, step):
                copy.wait_recv()
            for copy in passing(i, own - 4 * step):
                copy.start()

    other = HALO + 2 * (1 - core)
    for copy in taken(6, other):
        copy.wait_recv()
    for i, step in enumerate(steps):
        @pl.when(has(-step))
        def _():
            for copy in taken(i, other - 4 * step):
                copy.wait_recv()

    pole_here = order_ref[core]
    shift = shift_ref[pole_here]
    weight = weight_ref[pole_here]

    row = lax.broadcasted_iota(jnp.int32, (NY, NZ), 0)
    col = lax.broadcasted_iota(jnp.int32, (NY, NZ), 1)
    row_first, row_last = row == 0, row == NY - 1
    col_first, col_last = col == 0, col == NZ - 1
    row_odd, col_odd = lax.rem(row, 2) == 1, lax.rem(col, 2) == 1

    def inside(i):
        plane = 4 * chip + i - HALO
        return jnp.logical_and(plane >= 0, plane < 4 * chips)

    def fine_faces(i, odd):
        k = kap[i]
        fx, bx = 0.5 * (k + kap[i + 1]), 0.5 * (k + kap[i - 1])
        up_y = jnp.where(row_last, 0.0, roll(k, -1, 0))
        down_y = jnp.where(row_first, 0.0, roll(k, 1, 0))
        up_z = jnp.where(col_last, 0.0, roll(k, -1, 1))
        down_z = jnp.where(col_first, 0.0, roll(k, 1, 1))
        py, qy = 0.5 * (k + up_y), 0.5 * (k + down_y)
        pz, qz = 0.5 * (k + up_z), 0.5 * (k + down_z)
        d = shift + (fx + bx + (py + qy) + (pz + qz))
        g = jnp.where(inside(i), W, 0.0) / d
        my, mz = jnp.where(row_last, 0.0, py), jnp.where(col_last, 0.0, pz)
        face_x[i] = fx
        face_y[i] = my
        face_z[i] = mz
        diag[i] = d
        gain[i] = g
        z1[i] = g * res[i]
        block = shift + (fx if odd else bx) + jnp.where(row_odd, py, qy) + jnp.where(col_odd, pz, qz)
        return fx, block, jnp.where(row_odd, my, 0.0), jnp.where(col_odd, mz, 0.0)

    face_x[0] = 0.5 * (kap[0] + kap[1])
    fine_faces(1, True)
    fine_faces(PLANES - 2, False)

    def faces(j, carry):
        i = 2 * j
        _, block0, fy0, fz0 = fine_faces(i, False)
        fx, block1, fy1, fz1 = fine_faces(i + 1, True)
        cface_x[j] = pair_sum(fx)
        cface_y[j] = pair_sum(fy0 + fy1)
        cface_z[j] = pair_sum(fz0 + fz1)
        cgain[j] = jnp.where(inside(i), W, 0.0) / pair_sum(block0 + block1)
        return carry

    lax.fori_loop(1, PLANES // 2 - 1, faces, 0)

    def off(ref, i):
        v = ref[i]
        fy, fz = face_y[i], face_z[i]
        total = face_x[i] * ref[i + 1] + face_x[i - 1] * ref[i - 1]
        total = total + (fy * roll(v, -1, 0) + roll(fy * v, 1, 0))
        return total + (fz * roll(v, -1, 1) + roll(fz * v, 1, 1))

    def coarse_off(j):
        v = y1[j]
        fy, fz = cface_y[j], cface_z[j]
        total = cface_x[j] * y1[j + 1] + cface_x[j - 1] * y1[j - 1]
        total = total + (fy * roll(v, -2, 0) + roll(fy * v, 2, 0))
        return total + (fz * roll(v, -2, 1) + roll(fz * v, 2, 1))

    def precondition(source, out, lo, hi):
        def down(j, carry):
            i = 2 * j
            t = 0.2 * (source[i] + source[i + 1]) + (off(z1, i) + off(z1, i + 1))
            y1[j] = cgain[j] * pair_sum(t)
            return carry

        def up(j, carry):
            i = 2 * j
            y2 = 1.2 * y1[j] + cgain[j] * coarse_off(j)
            y2 = jnp.where(col_odd, roll(y2, 1, 1), y2)
            y2 = jnp.where(row_odd, roll(y2, 1, 0), y2)
            z2[i] = z1[i] + y2
            z2[i + 1] = z1[i + 1] + y2
            return carry

        def smooth(i, carry):
            out[i] = 0.2 * z2[i] + z1[i] + gain[i] * off(z2, i)
            return carry

        first, last = (lo - 1) // 2, hi // 2
        lax.fori_loop(first - 1, last + 2, down, 0)
        lax.fori_loop(first, last + 1, up, 0)
        lax.fori_loop(lo, hi, smooth, 0)

    precondition(res, u0, HALO - 6, HALO + 10)

    def residual(i, carry):
        value = res[i] - (diag[i] * u0[i] - off(u0, i))
        rt[i] = value
        z1[i] = gain[i] * value
        return carry

    lax.fori_loop(HALO - 5, HALO + 9, residual, 0)
    precondition(rt, ut, HALO - 1, HALO + 5)

    window = HALO - 1 + 2 * core
    sib_window = HALO + 1 - 2 * core
    swaps = [
        remote(u0.at[pl.ds(sib_window, 4)], sib_u, xs_send.at[0], xs_recv.at[0], near(sibling)),
        remote(ut.at[pl.ds(sib_window, 4)], sib_t, xs_send.at[1], xs_recv.at[1], near(sibling)),
    ]
    for copy in swaps:
        copy.start()

    def products(i, carry):
        g0, d0, e1, m0 = carry
        u, t, r, q = u0[i], rt[i], res[i], ut[i]
        image = diag[i] * q - off(ut, i)
        fold = lambda v: jnp.sum(v.reshape(NY // 8, 8, NZ), axis=0)
        return (g0 + fold(u * r), d0 + fold(u * t), e1 + fold(t * q), m0 + fold(q * image))

    zero = jnp.zeros((8, NZ), jnp.float32)
    totals = lax.fori_loop(HALO, HALO + 4, products, (zero,) * 4)
    sub = lax.broadcasted_iota(jnp.int32, (8, NZ), 0)
    tile = zero
    for k, total in enumerate(totals):
        tile = jnp.where(sub == k, jnp.sum(total, axis=0, keepdims=True), tile)
    part[0] = tile

    def reduce_copy(d):
        return remote(part.at[0], part.at[d], ar_send, ar_recv,
                      near(lax.rem(space + 2 * d, 2 * chips)))

    def reduce_start(d, carry):
        reduce_copy(d).start()
        return carry

    lax.fori_loop(1, chips, reduce_start, 0)
    everyone = pltpu.make_async_copy(part.at[pl.ds(1, chips - 1)], part.at[pl.ds(1, chips - 1)], ar_recv)
    everyone.wait()
    total = jnp.sum(part[...], axis=0)
    total = jnp.sum(total, axis=1, keepdims=True)
    lane = lax.broadcasted_iota(jnp.int32, (8, NZ), 1)

    g0, d0, e1, m0 = (total[k : k + 1] for k in range(4))
    c0 = g0 - d0
    eta = d0 / c0
    a0 = 1.0 + eta
    t = d0 - e1
    k = c0 - t
    g1 = e1 - 2.0 * eta * t + eta * eta * k
    b = g1 / g0
    s11 = m0 - 2.0 * eta * (t - m0) + eta * eta * (k - t + m0)
    c1 = s11 + 2.0 * b * (t - eta * k) + b * b * c0
    a1 = g1 / c1
    first = weight * (a0 + a1 * (b - eta))
    second = weight * (a1 * a0)
    sums[...] = jnp.where(lane == 0, first, second)
    scalars = remote(sums, swap, sw_send, sw_recv, near(sibling))
    scalars.start()
    for copy in swaps:
        copy.wait_recv()

    def combine(source_u, source_t, at, slot, one, two):
        for n in range(4):
            xout[slot, n] = one * source_u[at + n] + two * source_t[at + n]

    combine(u0, ut, window, core, first, second)
    scalars.wait_recv()
    combine(sib_u, sib_t, 0, 1 - core, swap[0:1, 0:1], swap[0:1, 1:2])
    adjoint_out = pltpu.make_async_copy(xout.at[:, pl.ds(1, 2)], adjoint_ref, loc.at[3])
    adjoint_out.start()

    @pl.when(space > 0)
    def _():
        to_following.wait_recv()

    @pl.when(space < 2 * chips - 1)
    def _():
        to_previous.wait_recv()

    def side(x, f, axis, first_mask, last_mask):
        forward = (x - jnp.where(last_mask, 0.0, roll(x, -1, axis))) * (
            f - jnp.where(last_mask, 0.0, roll(f, -1, axis))
        )
        return forward + jnp.where(first_mask, x * f, roll(forward, 1, axis))

    def terms(n, carry):
        total = jnp.zeros((NY, NZ), jnp.float32)
        for slot in range(2):
            x, f = xout[slot, n], fwd[slot, n]
            total = total + (x - xout[slot, n + 1]) * (f - fwd[slot, n + 1])
            total = total + (x - xout[slot, n - 1]) * (f - fwd[slot, n - 1])
            total = total + side(x, f, 0, row_first, row_last) + side(x, f, 1, col_first, col_last)
        term[n - 1] = -0.5 * total
        return carry

    lax.fori_loop(1, 3, terms, 0)

    def rows(q):
        return term.at[:, pl.ds(pl.multiple_of(8 * q, 8), 8), :]

    spread = []
    for d in range(1, poles):
        q = lax.rem(pole + d, poles)
        spread.append(remote(rows(q), pieces.at[d], rs_send.at[d], rs_recv.at[d], (q, space)))
    for copy in spread:
        copy.start()
    total = term[:, pl.ds(pl.multiple_of(8 * pole, 8), 8), :]
    for d, copy in enumerate(spread):
        copy.wait_recv()
        total = total + pieces[d + 1]
    gout[...] = total
    gradient_out = pltpu.make_async_copy(gout, gradient_ref, loc.at[4])
    gradient_out.start()

    for i, step in enumerate(steps):
        @pl.when(has(step))
        def _():
            for copy in outgoing(i, step):
                copy.wait_send()

        @pl.when(has(-step))
        def _():
            for copy in passing(i, own - 4 * step):
                copy.wait_send()
    for copy in passing(6, own):
        copy.wait_send()

    @pl.when(space > 0)
    def _():
        to_previous.wait_send()

    @pl.when(space < 2 * chips - 1)
    def _():
        to_following.wait_send()

    for copy in swaps:
        copy.wait_send()
    pltpu.make_async_copy(part.at[pl.ds(1, chips - 1)], part.at[pl.ds(1, chips - 1)], ar_send).wait()
    scalars.wait_send()
    for copy in spread:
        copy.wait_send()
    adjoint_out.wait()
    gradient_out.wait()


def solution(mesh):
    chips, poles = mesh.shape["space"] // 2, mesh.shape["pole"]
    f32 = jnp.float32

    def per_device(conductivity, misfit, forward_states, pole_shifts, pole_weights, pole_order):
        smem = pl.BlockSpec(memory_space=pltpu.SMEM)
        hbm = pl.BlockSpec(memory_space=pl.ANY)
        fine = pltpu.VMEM((PLANES, NY, NZ), f32)
        coarse = pltpu.VMEM((PLANES // 2, NY, NZ), f32)
        window = pltpu.VMEM((4, NY, NZ), f32)
        dma = pltpu.SemaphoreType.DMA
        return pl.pallas_call(
            functools.partial(kernel, chips, poles),
            out_shape=(
                jax.ShapeDtypeStruct(forward_states.shape, f32),
                jax.ShapeDtypeStruct((2, NY // poles, NZ), f32),
            ),
            in_specs=[smem, smem, smem, hbm, hbm, hbm],
            out_specs=(hbm, hbm),
            scratch_shapes=[fine] * 12 + [coarse] * 5 + [
                pltpu.VMEM((2, 4, NY, NZ), f32), window, window, pltpu.VMEM((2, 4, NY, NZ), f32),
                pltpu.VMEM((chips, 8, NZ), f32), pltpu.VMEM((8, NZ), f32), pltpu.VMEM((8, NZ), f32),
                pltpu.VMEM((2, NY, NZ), f32), pltpu.VMEM((poles, 2, NY // poles, NZ), f32),
                pltpu.VMEM((2, NY // poles, NZ), f32),
                dma((2, 6)), dma((2, 6)), dma((2, 7)), dma((2, 7)), dma((2,)), dma((2,)), dma((5,)),
                dma, dma, dma, dma, dma((2,)), dma((2,)), dma((poles,)), dma((poles,)),
            ],
            compiler_params=pltpu.CompilerParams(
                collective_id=0, has_side_effects=True, vmem_limit_bytes=40 << 20
            ),
            name="adjoint_gradient",
        )(pole_shifts, pole_weights, pole_order, conductivity, misfit, forward_states)

    in_specs = (
        P("space", None, None), P("space", None, None), P("pole", "space", None, None),
        P(), P(), P("pole"),
    )
    out_specs = (P("pole", "space", None, None), P("space", "pole", None))
    return jax.shard_map(per_device, mesh=mesh, in_specs=in_specs, out_specs=out_specs, check_vma=False)
```

time: 1190 us -> 69.2 us (0.06)
  blocking collectives: 839 us -> 0 us
  starting transfers between devices: 117 us -> 0 us
  waiting for transfers between devices: 103 us -> 0 us
  Pallas kernels: 0 us -> 62.4 us
  other arithmetic: 51 us -> 0 us
  local copies, waits for them, and re-layouts: 52.8 us -> 5.8 us
  between operations: 23.9 us -> 0.65 us
    psum x4 -> x0, blocking collectives: 839 us -> none  [the longest x3 629 us: norm_sum(): return lax.psum(cell_sums(residual * precond), 'space')]
    ppermute x36 -> x0, starting transfers between devices: 117 us -> none  [the longest x18 58.6 us: extended(): after = lax.ppermute(leading, axis, down)]
    reduce_scatter x1 -> x0, waiting for transfers between devices: 94.7 us -> none  [per_device(): lax.psum_scatter(local_term, 'pole', scatter_dimension=1, tiled=True)]
    pallas_call x0 -> x1, Pallas kernels: none -> 62.4 us  [per_device(): pl.pallas_call(functools.partial(kernel, chips, poles), out_shape=(jax.Sh...]
    reduce_sum x21 -> x0, other arithmetic: 33.6 us -> none  [the longest x6 14 us: coarse_pick(): return jnp.sum(chosen, axis=(1, 3, 5))]
    reshape x6 -> x0, local copies, waits for them, and re-layouts: 33.1 us -> none  [coarse_pick(): blocks = faces.reshape(extent_x // 2, 2, extent_y // 2, 2, extent_z // 2, 2)]
  transfers between devices with their start and end apart: 37 -> 0, of which waited for: 10 -> 0; matrix products, arithmetic and copies ran while one was open for 6% -> 0% of each run, Pallas kernels for 0% -> 0%
where the time goes in v1:
time: 69.2 us; the launch traced here: 68.8 us
  Pallas kernels  62.4 us (90%)
  local copies, waits for them, and re-layouts  5.8 us (8%)
    pallas_call x1, Pallas kernels, per_device(): pl.pallas_call(functools.partial(kernel, chips, poles), out_shape=(jax.Sh...  62.4 us
    unnamed x14, local copies, waits for them, and re-layouts  5.8 us

profile of v1, /device:TPU:1, one launch (start us, length us, event | category | flops | bytes accessed | tf_op | source)
XLA Modules:
  0.0 68.8 jit_solution(11320138890753095517)
XLA Ops:
  0.6 0.0 copy-start
  0.6 0.9 %copy-done = f32[2,2,64,128]{3,2,1,0:T(8,128)S(1)} copy-done((f32[2,2,64,128]{3,2,1,0:T(8,128)S(1)}, f32[2,2,64,128]{3,2,1,0:T(8,128)}, u32[]{:S(2)}) %copy-start) | copy-done | bytes 131096
  1.5 0.0 copy-start.1
  1.5 0.8 %copy-done.1 = f32[2,64,128]{2,1,0:T(8,128)S(1)} copy-done((f32[2,64,128]{2,1,0:T(8,128)S(1)}, f32[2,64,128]{2,1,0:T(8,128)}, u32[]{:S(2)}) %copy-start.1) | copy-done | bytes 65560
  2.4 0.0 copy-start.2
  2.4 0.8 %copy-done.2 = f32[2,64,128]{2,1,0:T(8,128)S(1)} copy-done((f32[2,64,128]{2,1,0:T(8,128)S(1)}, f32[2,64,128]{2,1,0:T(8,128)}, u32[]{:S(2)}) %copy-start.2) | copy-done | bytes 65560
  3.2 0.0 copy-start.3
  3.2 0.7 copy-done.3
  3.9 0.0 copy-start.4
  3.9 0.7 copy-done.4
  4.5 0.0 copy-start.5
  4.5 0.7 copy-done.5
  5.2 62.4 %adjoint_gradient.1 = (f32[2,2,64,128]{3,2,1,0:T(8,128)S(1)}, f32[2,8,128]{2,1,0:T(8,128)S(1)}) custom-call(f32[16]{0:T(128)S(1)} %copy-done.3, f32[16]{0:T(128)S(1)} %copy-done.4, s32[2]{0:T(128)S(1)} %copy-done.5, f32[2,64,128]{2,1,0:T(8,128)S(1)} %copy-done.1, f32[2,64,128]{2,1,0:T(8,128)S(1)} %copy-done.2, f32[2,2,64,128]{3,2,1,0:T(8,128)S(1)} %copy-done), custom_call_target="tpu_custom_call" | custom-call | tf_op jit(solution)/shard_map/adjoint_gradient/pallas_call | solution.py:425
  67.6 0.7 copy.10
  68.2 0.6 copy.11
Async XLA Ops:
  0.6 0.9 %copy-start = (f32[2,2,64,128]{3,2,1,0:T(8,128)S(1)}, f32[2,2,64,128]{3,2,1,0:T(8,128)}, u32[]{:S(2)}) copy-start(f32[2,2,64,128]{3,2,1,0:T(8,128)} %forward_ref.1) | copy-start | bytes 393220
  1.5 0.8 %copy-start.1 = (f32[2,64,128]{2,1,0:T(8,128)S(1)}, f32[2,64,128]{2,1,0:T(8,128)}, u32[]{:S(2)}) copy-start(f32[2,64,128]{2,1,0:T(8,128)} %kappa_ref.1) | copy-start | bytes 196612
  2.4 0.8 %copy-start.2 = (f32[2,64,128]{2,1,0:T(8,128)S(1)}, f32[2,64,128]{2,1,0:T(8,128)}, u32[]{:S(2)}) copy-start(f32[2,64,128]{2,1,0:T(8,128)} %misfit_ref.1) | copy-start | bytes 196612
  3.2 0.7 copy-start.3
  3.9 0.7 copy-start.4
  4.5 0.7 copy-start.5

commit v2 on v1

--- a/solution.py
+++ b/solution.py
@@ -9,6 +9,7 @@
 
 MESH = pl.DeviceIdType.MESH
 W = 0.8
+UNROLL_F, UNROLL_D, UNROLL_U, UNROLL_S, UNROLL_R = 4, True, True, True, True
 NY, NZ = 64, 128
 HALO = 12
 PLANES = 4 + 2 * HALO
@@ -18,18 +19,45 @@
     return pltpu.roll(value, shift % value.shape[axis], axis)
 
 
+def next_row(value):
+    return jnp.concatenate([value[1:], roll(value[:1], -1, 1)], axis=0)
+
+
+def previous_row(value):
+    return jnp.concatenate([roll(value[-1:], 1, 1), value[:-1]], axis=0)
+
+
+def rows_of(value):
+    pairs = value.reshape(value.shape[0] // 2, 2, *value.shape[1:])
+    return pairs[:, 0], pairs[:, 1]
+
+
+def row_pairs(value):
+    even, odd = rows_of(value)
+    return even + odd
+
+
 def pair_sum(value):
-    value = value + roll(value, -1, 1)
-    return value + roll(value, -1, 0)
+    value = row_pairs(value)
+    return value + roll(value, -1, 2)
+
+
+def natural(ref, index):
+    return jnp.stack([ref[(*index, pl.ds(v, 8, stride=8), slice(None))] for v in range(8)])
+
+
+def put_natural(ref, index, value):
+    for v in range(8):
+        ref[(*index, pl.ds(v, 8, stride=8), slice(None))] = value[v]
 
 
 def kernel(
     chips, poles,
     shift_ref, weight_ref, order_ref, kappa_ref, misfit_ref, forward_ref,
     adjoint_ref, gradient_ref,
-    kap, res, face_x, face_y, face_z, diag, gain, z1, z2, u0, rt, ut,
+    shift_mem, weight_mem, order_mem, kap, res, face_x, face_y, face_z, diag, gain, z1, z2, u0, rt, ut,
     cgain, cface_x, cface_y, cface_z, y1,
-    fwd, sib_u, sib_t, xout, part, sums, swap, term, pieces, gout,
+    stage, fwd, sib_u, sib_t, xout, xnat, part, sums, swap, term, pieces, gout,
     near_send, near_recv, sib_send, sib_recv, f_send, f_recv, loc, ar_send, ar_recv, sw_send, sw_recv,
     xs_send, xs_recv, rs_send, rs_recv,
 ):
@@ -69,26 +97,37 @@
 
     own = HALO + 2 * core
     own_copies = [
-        pltpu.make_async_copy(kappa_ref, kap.at[pl.ds(own, 2)], loc.at[0]),
-        pltpu.make_async_copy(misfit_ref, res.at[pl.ds(own, 2)], loc.at[1]),
-        pltpu.make_async_copy(forward_ref, fwd.at[:, pl.ds(1, 2)], loc.at[2]),
+        pltpu.make_async_copy(kappa_ref, stage.at[0], loc.at[0]),
+        pltpu.make_async_copy(misfit_ref, stage.at[1], loc.at[1]),
+        pltpu.make_async_copy(forward_ref, stage.at[pl.ds(2, 2)], loc.at[2]),
+        pltpu.make_async_copy(shift_ref, shift_mem, loc.at[3]),
+        pltpu.make_async_copy(weight_ref, weight_mem, loc.at[4]),
+        pltpu.make_async_copy(order_ref, order_mem, loc.at[5]),
     ]
     for copy in own_copies:
         copy.start()
     for step in steps:
         @pl.when(jnp.logical_not(has(step)))
         def _():
-            zeros = jnp.zeros((4, NY, NZ), jnp.float32)
+            zeros = jnp.zeros((4, 8, 8, NZ), jnp.float32)
             kap[pl.ds(HALO + 4 * step, 4)] = zeros
             res[pl.ds(HALO + 4 * step, 4)] = zeros
 
     @pl.when(space == 0)
     def _():
-        fwd[:, 0] = jnp.zeros((2, NY, NZ), jnp.float32)
+        fwd[:, 0] = jnp.zeros((2, 8, 8, NZ), jnp.float32)
 
     @pl.when(space == 2 * chips - 1)
     def _():
-        fwd[:, 3] = jnp.zeros((2, NY, NZ), jnp.float32)
+        fwd[:, 3] = jnp.zeros((2, 8, 8, NZ), jnp.float32)
+
+    for copy in own_copies:
+        copy.wait()
+    for n in range(2):
+        kap[own + n] = natural(stage, (0, n))
+        res[own + n] = natural(stage, (1, n))
+        for slot in range(2):
+            fwd[slot, 1 + n] = natural(stage, (2 + slot, n))
 
     pl.semaphore_wait(barrier, chips + poles - 1 + has_across.astype(jnp.int32))
 
@@ -101,17 +140,17 @@
     def outgoing(i, step):
         at = own - 4 * step
         return [
-            remote(source, dest.at[pl.ds(at, 2)], near_send.at[a, i], near_recv.at[a, i],
+            remote(dest.at[pl.ds(own, 2)], dest.at[pl.ds(at, 2)], near_send.at[a, i], near_recv.at[a, i],
                    near(space + 2 * step))
-            for a, (source, dest) in enumerate(((kappa_ref, kap), (misfit_ref, res)))
+            for a, dest in enumerate((kap, res))
         ]
 
     def incoming(i, step):
         at = own - 4 * step
         return [
-            remote(source, dest.at[pl.ds(at, 2)], near_send.at[a, i], near_recv.at[a, i],
+            remote(dest.at[pl.ds(own, 2)], dest.at[pl.ds(at, 2)], near_send.at[a, i], near_recv.at[a, i],
                    near(space - 2 * step))
-            for a, (source, dest) in enumerate(((kappa_ref, kap), (misfit_ref, res)))
+            for a, dest in enumerate((kap, res))
         ]
 
     def passing(i, at):
@@ -134,14 +173,12 @@
             for copy in outgoing(i, step):
                 copy.start()
 
-    for copy in own_copies:
-        copy.wait()
     for copy in passing(6, own):
         copy.start()
 
     previous, following = space - 1, space + 1
-    to_previous = remote(forward_ref.at[:, 0], fwd.at[:, 3], f_send.at[0], f_recv.at[0], near(previous))
-    to_following = remote(forward_ref.at[:, 1], fwd.at[:, 0], f_send.at[1], f_recv.at[1], near(following))
+    to_previous = remote(fwd.at[:, 1], fwd.at[:, 3], f_send.at[0], f_recv.at[0], near(previous))
+    to_following = remote(fwd.at[:, 2], fwd.at[:, 0], f_send.at[1], f_recv.at[1], near(following))
 
     @pl.when(space > 0)
     def _():
@@ -168,15 +205,16 @@
             for copy in taken(i, other - 4 * step):
                 copy.wait_recv()
 
-    pole_here = order_ref[core]
-    shift = shift_ref[pole_here]
-    weight = weight_ref[pole_here]
-
-    row = lax.broadcasted_iota(jnp.int32, (NY, NZ), 0)
-    col = lax.broadcasted_iota(jnp.int32, (NY, NZ), 1)
+    pole_here = order_mem[core]
+    shift = shift_mem[pole_here]
+    weight = weight_mem[pole_here]
+
+    block = (8, 8, NZ)
+    row = 8 * lax.broadcasted_iota(jnp.int32, block, 1) + lax.broadcasted_iota(jnp.int32, block, 0)
+    col = lax.broadcasted_iota(jnp.int32, block, 2)
     row_first, row_last = row == 0, row == NY - 1
     col_first, col_last = col == 0, col == NZ - 1
-    row_odd, col_odd = lax.rem(row, 2) == 1, lax.rem(col, 2) == 1
+    col_odd = lax.rem(lax.broadcasted_iota(jnp.int32, (4, 8, NZ), 2), 2) == 1
 
     def inside(i):
         plane = 4 * chip + i - HALO
@@ -185,10 +223,10 @@
     def fine_faces(i, odd):
         k = kap[i]
         fx, bx = 0.5 * (k + kap[i + 1]), 0.5 * (k + kap[i - 1])
-        up_y = jnp.where(row_last, 0.0, roll(k, -1, 0))
-        down_y = jnp.where(row_first, 0.0, roll(k, 1, 0))
-        up_z = jnp.where(col_last, 0.0, roll(k, -1, 1))
-        down_z = jnp.where(col_first, 0.0, roll(k, 1, 1))
+        up_y = jnp.where(row_last, 0.0, next_row(k))
+        down_y = jnp.where(row_first, 0.0, previous_row(k))
+        up_z = jnp.where(col_last, 0.0, roll(k, -1, 2))
+        down_z = jnp.where(col_first, 0.0, roll(k, 1, 2))
         py, qy = 0.5 * (k + up_y), 0.5 * (k + down_y)
         pz, qz = 0.5 * (k + up_z), 0.5 * (k + down_z)
         d = shift + (fx + bx + (py + qy) + (pz + qz))
@@ -200,8 +238,8 @@
         diag[i] = d
         gain[i] = g
         z1[i] = g * res[i]
-        block = shift + (fx if odd else bx) + jnp.where(row_odd, py, qy) + jnp.where(col_odd, pz, qz)
-        return fx, block, jnp.where(row_odd, my, 0.0), jnp.where(col_odd, mz, 0.0)
+        around = row_pairs(shift + (fx if odd else bx)), rows_of(qy)[0] + rows_of(py)[1], row_pairs(pz), row_pairs(qz)
+        return fx, around, rows_of(my)[1], row_pairs(mz)
 
     face_x[0] = 0.5 * (kap[0] + kap[1])
     fine_faces(1, True)
@@ -209,29 +247,32 @@
 
     def faces(j, carry):
         i = 2 * j
-        _, block0, fy0, fz0 = fine_faces(i, False)
-        fx, block1, fy1, fz1 = fine_faces(i + 1, True)
+        _, (bx0, by0, pz0, qz0), fy0, fz0 = fine_faces(i, False)
+        fx, (bx1, by1, pz1, qz1), fy1, fz1 = fine_faces(i + 1, True)
         cface_x[j] = pair_sum(fx)
-        cface_y[j] = pair_sum(fy0 + fy1)
-        cface_z[j] = pair_sum(fz0 + fz1)
-        cgain[j] = jnp.where(inside(i), W, 0.0) / pair_sum(block0 + block1)
+        fy = fy0 + fy1
+        cface_y[j] = fy + roll(fy, -1, 2)
+        cface_z[j] = roll(fz0 + fz1, -1, 2)
+        both = (bx0 + bx1) + (by0 + by1)
+        d = both + (qz0 + qz1) + roll(both + (pz0 + pz1), -1, 2)
+        cgain[j] = jnp.where(inside(i), W, 0.0) / d
         return carry
 
-    lax.fori_loop(1, PLANES // 2 - 1, faces, 0)
+    lax.fori_loop(1, PLANES // 2 - 1, faces, 0, unroll=UNROLL_F)
 
     def off(ref, i):
         v = ref[i]
         fy, fz = face_y[i], face_z[i]
         total = face_x[i] * ref[i + 1] + face_x[i - 1] * ref[i - 1]
-        total = total + (fy * roll(v, -1, 0) + roll(fy * v, 1, 0))
-        return total + (fz * roll(v, -1, 1) + roll(fz * v, 1, 1))
+        total = total + (fy * next_row(v) + previous_row(fy * v))
+        return total + (fz * roll(v, -1, 2) + roll(fz * v, 1, 2))
 
     def coarse_off(j):
         v = y1[j]
         fy, fz = cface_y[j], cface_z[j]
         total = cface_x[j] * y1[j + 1] + cface_x[j - 1] * y1[j - 1]
-        total = total + (fy * roll(v, -2, 0) + roll(fy * v, 2, 0))
-        return total + (fz * roll(v, -2, 1) + roll(fz * v, 2, 1))
+        total = total + (fy * next_row(v) + previous_row(fy * v))
+        return total + (fz * roll(v, -2, 2) + roll(fz * v, 2, 2))
 
     def precondition(source, out, lo, hi):
         def down(j, carry):
@@ -243,8 +284,8 @@
         def up(j, carry):
             i = 2 * j
             y2 = 1.2 * y1[j] + cgain[j] * coarse_off(j)
-            y2 = jnp.where(col_odd, roll(y2, 1, 1), y2)
-            y2 = jnp.where(row_odd, roll(y2, 1, 0), y2)
+            y2 = jnp.where(col_odd, roll(y2, 1, 2), y2)
+            y2 = jnp.stack([y2, y2], axis=1).reshape(8, 8, NZ)
             z2[i] = z1[i] + y2
             z2[i + 1] = z1[i + 1] + y2
             return carry
@@ -254,9 +295,9 @@
             return carry
 
         first, last = (lo - 1) // 2, hi // 2
-        lax.fori_loop(first - 1, last + 2, down, 0)
-        lax.fori_loop(first, last + 1, up, 0)
-        lax.fori_loop(lo, hi, smooth, 0)
+        lax.fori_loop(first - 1, last + 2, down, 0, unroll=UNROLL_D)
+        lax.fori_loop(first, last + 1, up, 0, unroll=UNROLL_U)
+        lax.fori_loop(lo, hi, smooth, 0, unroll=UNROLL_S)
 
     precondition(res, u0, HALO - 6, HALO + 10)
 
@@ -266,7 +307,7 @@
         z1[i] = gain[i] * value
         return carry
 
-    lax.fori_loop(HALO - 5, HALO + 9, residual, 0)
+    lax.fori_loop(HALO - 5, HALO + 9, residual, 0, unroll=UNROLL_R)
     precondition(rt, ut, HALO - 1, HALO + 5)
 
     window = HALO - 1 + 2 * core
@@ -282,7 +323,7 @@
         g0, d0, e1, m0 = carry
         u, t, r, q = u0[i], rt[i], res[i], ut[i]
         image = diag[i] * q - off(ut, i)
-        fold = lambda v: jnp.sum(v.reshape(NY // 8, 8, NZ), axis=0)
+        fold = lambda v: jnp.sum(v, axis=0)
         return (g0 + fold(u * r), d0 + fold(u * t), e1 + fold(t * q), m0 + fold(q * image))
 
     zero = jnp.zeros((8, NZ), jnp.float32)
@@ -334,7 +375,10 @@
     combine(u0, ut, window, core, first, second)
     scalars.wait_recv()
     combine(sib_u, sib_t, 0, 1 - core, swap[0:1, 0:1], swap[0:1, 1:2])
-    adjoint_out = pltpu.make_async_copy(xout.at[:, pl.ds(1, 2)], adjoint_ref, loc.at[3])
+    for slot in range(2):
+        for n in range(2):
+            put_natural(xnat, (slot, n), xout[slot, 1 + n])
+    adjoint_out = pltpu.make_async_copy(xnat, adjoint_ref, loc.at[3])
     adjoint_out.start()
 
     @pl.when(space > 0)
@@ -345,20 +389,24 @@
     def _():
         to_previous.wait_recv()
 
-    def side(x, f, axis, first_mask, last_mask):
-        forward = (x - jnp.where(last_mask, 0.0, roll(x, -1, axis))) * (
-            f - jnp.where(last_mask, 0.0, roll(f, -1, axis))
-        )
-        return forward + jnp.where(first_mask, x * f, roll(forward, 1, axis))
+    def ahead_row(v):
+        return jnp.where(row_last, 0.0, next_row(v))
+
+    def ahead_col(v):
+        return jnp.where(col_last, 0.0, roll(v, -1, 2))
 
     def terms(n, carry):
-        total = jnp.zeros((NY, NZ), jnp.float32)
+        total = jnp.zeros(block, jnp.float32)
         for slot in range(2):
             x, f = xout[slot, n], fwd[slot, n]
             total = total + (x - xout[slot, n + 1]) * (f - fwd[slot, n + 1])
             total = total + (x - xout[slot, n - 1]) * (f - fwd[slot, n - 1])
-            total = total + side(x, f, 0, row_first, row_last) + side(x, f, 1, col_first, col_last)
-        term[n - 1] = -0.5 * total
+            product = x * f
+            ahead = (x - ahead_row(x)) * (f - ahead_row(f))
+            total = total + ahead + jnp.where(row_first, product, previous_row(ahead))
+            ahead = (x - ahead_col(x)) * (f - ahead_col(f))
+            total = total + ahead + jnp.where(col_first, product, roll(ahead, 1, 2))
+        put_natural(term, (n - 1,), -0.5 * total)
         return carry
 
     lax.fori_loop(1, 3, terms, 0)
@@ -416,11 +464,11 @@
     f32 = jnp.float32
 
     def per_device(conductivity, misfit, forward_states, pole_shifts, pole_weights, pole_order):
-        smem = pl.BlockSpec(memory_space=pltpu.SMEM)
-        hbm = pl.BlockSpec(memory_space=pl.ANY)
-        fine = pltpu.VMEM((PLANES, NY, NZ), f32)
-        coarse = pltpu.VMEM((PLANES // 2, NY, NZ), f32)
-        window = pltpu.VMEM((4, NY, NZ), f32)
+        hbm = pl.BlockSpec(memory_space=pltpu.HBM)
+        fine = pltpu.VMEM((PLANES, 8, 8, NZ), f32)
+        coarse = pltpu.VMEM((PLANES // 2, 4, 8, NZ), f32)
+        window = pltpu.VMEM((4, 8, 8, NZ), f32)
+        windows = pltpu.VMEM((2, 4, 8, 8, NZ), f32)
         dma = pltpu.SemaphoreType.DMA
         return pl.pallas_call(
             functools.partial(kernel, chips, poles),
@@ -428,18 +476,21 @@
                 jax.ShapeDtypeStruct(forward_states.shape, f32),
                 jax.ShapeDtypeStruct((2, NY // poles, NZ), f32),
             ),
-            in_specs=[smem, smem, smem, hbm, hbm, hbm],
+            in_specs=[hbm] * 6,
             out_specs=(hbm, hbm),
-            scratch_shapes=[fine] * 12 + [coarse] * 5 + [
-                pltpu.VMEM((2, 4, NY, NZ), f32), window, window, pltpu.VMEM((2, 4, NY, NZ), f32),
+            scratch_shapes=[pltpu.SMEM(pole_shifts.shape, f32), pltpu.SMEM(pole_weights.shape, f32),
+                            pltpu.SMEM(pole_order.shape, jnp.int32)]
+            + [fine] * 12 + [coarse] * 5 + [
+                pltpu.VMEM((4, 2, NY, NZ), f32), windows, window, window, windows,
+                pltpu.VMEM((2, 2, NY, NZ), f32),
                 pltpu.VMEM((chips, 8, NZ), f32), pltpu.VMEM((8, NZ), f32), pltpu.VMEM((8, NZ), f32),
                 pltpu.VMEM((2, NY, NZ), f32), pltpu.VMEM((poles, 2, NY // poles, NZ), f32),
                 pltpu.VMEM((2, NY // poles, NZ), f32),
-                dma((2, 6)), dma((2, 6)), dma((2, 7)), dma((2, 7)), dma((2,)), dma((2,)), dma((5,)),
+                dma((2, 6)), dma((2, 6)), dma((2, 7)), dma((2, 7)), dma((2,)), dma((2,)), dma((6,)),
                 dma, dma, dma, dma, dma((2,)), dma((2,)), dma((poles,)), dma((poles,)),
             ],
             compiler_params=pltpu.CompilerParams(
-                collective_id=0, has_side_effects=True, vmem_limit_bytes=40 << 20
+                collective_id=0, has_side_effects=True, vmem_limit_bytes=64 << 20
             ),
             name="adjoint_gradient",
         )(pole_shifts, pole_weights, pole_order, conductivity, misfit, forward_states)

time: 69.2 us -> 59.2 us (0.86)
  Pallas kernels: 62.4 us -> 56.1 us
  local copies, waits for them, and re-layouts: 5.8 us -> 2.18 us
    pallas_call x1, Pallas kernels: 62.4 us -> 56.1 us  [per_device(): pl.pallas_call(functools.partial(kernel, chips, poles), out_shape=(jax.Sh...]
    unnamed x14 -> x4, local copies, waits for them, and re-layouts: 5.8 us -> 2.18 us
where the time goes in v2:
time: 59.2 us; the launch traced here: 58.9 us
  Pallas kernels  56.1 us (95%)
  local copies, waits for them, and re-layouts  2.18 us (4%)
  between operations  0.65 us (1%)
    pallas_call x1, Pallas kernels, per_device(): pl.pallas_call(functools.partial(kernel, chips, poles), out_shape=(jax.Sh...  56.1 us
    unnamed x4, local copies, waits for them, and re-layouts  2.18 us

profile of v2, /device:TPU:1, one launch (start us, length us, event | category | flops | bytes accessed | tf_op | source)
XLA Modules:
  0.0 58.9 jit_solution(3248563109809929142)
XLA Ops:
  0.6 56.1 %adjoint_gradient.1 = (f32[2,2,64,128]{3,2,1,0:T(8,128)}, f32[2,8,128]{2,1,0:T(8,128)}) custom-call(f32[16]{0:T(128)} %shift_ref.1, f32[16]{0:T(128)} %weight_ref.1, s32[2]{0:T(128)} %order_ref.1, f32[2,64,128]{2,1,0:T(8,128)} %kappa_ref.1, f32[2,64,128]{2,1,0:T(8,128)} %misfit_ref.1, f32[2,2,64,128]{3,2,1,0:T(8,128)} %forward_ref.1), custom_call_target="tpu_custom_call" | custom-call | tf_op jit(solution)/shard_map/adjoint_gradient/pallas_call | solution.py:473
  56.7 0.0 copy-start
  56.7 1.6 %copy.10 = f32[2,2,64,128]{3,2,1,0:T(8,128)} copy(f32[2,2,64,128]{3,2,1,0:T(8,128)} %get-tuple-element.4) | data formatting | bytes 262144
  58.3 0.0 copy-done
  58.3 0.6 %copy.11 = f32[2,8,128]{2,1,0:T(8,128)} copy(f32[2,8,128]{2,1,0:T(8,128)S(1)} %copy-done) | data formatting | bytes 16384
Async XLA Ops:
  56.7 1.6 %copy-start = (f32[2,8,128]{2,1,0:T(8,128)S(1)}, f32[2,8,128]{2,1,0:T(8,128)}, u32[]{:S(2)}) copy-start(f32[2,8,128]{2,1,0:T(8,128)} %get-tuple-element.5) | copy-start | bytes 24580

commit v3 on v2

v3 whole, which is shorter than its diff:
```python
import functools

import jax
import jax.numpy as jnp
from jax import lax
from jax.experimental import pallas as pl
from jax.experimental.pallas import tpu as pltpu
from jax.sharding import PartitionSpec as P

MESH = pl.DeviceIdType.MESH
W = 0.8
NY, NZ = 64, 128
HALO = 12
PLANES = 4 + 2 * HALO
TOKENS = (3, 6, 12, 24)
TOP = NY // 2 + 8


def roll(value, shift, axis):
    return pltpu.roll(value, shift % value.shape[axis], axis)


def next_row(value):
    return jnp.concatenate([value[1:], roll(value[:1], -1, 1)], axis=0)


def previous_row(value):
    return jnp.concatenate([roll(value[-1:], 1, 1), value[:-1]], axis=0)


def rows_of(value):
    pairs = value.reshape(value.shape[0] // 2, 2, *value.shape[1:])
    return pairs[:, 0], pairs[:, 1]


def row_pairs(value):
    even, odd = rows_of(value)
    return even + odd


def pair_sum(value):
    value = row_pairs(value)
    return value + roll(value, -1, 2)


def lane_sides(value, shifts):
    rows = value.reshape(-1, NZ)
    high = rows.astype(jnp.bfloat16)
    rest = rows - high.astype(jnp.float32)
    mid = rest.astype(jnp.bfloat16)
    low = (rest - mid.astype(jnp.float32)).astype(jnp.bfloat16)
    out = jnp.dot(jnp.concatenate([high, mid, low], axis=1), shifts, preferred_element_type=jnp.float32)
    return out[:, :NZ].reshape(value.shape), out[:, NZ:].reshape(value.shape)


def natural(ref, index):
    return jnp.stack([ref[(*index, pl.ds(v, 8, stride=8), slice(None))] for v in range(8)])


def put_natural(ref, index, value):
    for v in range(8):
        ref[(*index, pl.ds(v, 8, stride=8), slice(None))] = value[v]


def kernel(
    chips, poles,
    shift_ref, weight_ref, order_ref, kappa_ref, misfit_ref, forward_ref,
    adjoint_ref, gradient_ref,
    shift_mem, weight_mem, order_mem,
    kap, res, face_x, face_y, face_z, down_z, base, diag, gain, z1, z2, rt,
    cface_x, cface_y, cface_z, cbase, cgain, y1, u0, ut,
    sib_u, sib_t, fwd, xout, stage, stage_far, xnat, term, param, part, sums, swap, pieces, gout, gfar, gnear, shifts,
    loc, near_send, near_recv, sib_send, sib_recv, f_send, f_recv, ar_send, ar_recv, sw_send, sw_recv,
    xs_send, xs_recv, rs_send, rs_recv, far_send, far_recv, token,
):
    half_poles = poles // 2
    pole = lax.axis_index("pole")
    space = lax.axis_index("space")
    half, yy = pole // half_poles, lax.rem(pole, half_poles)
    early, late = half == 0, half == 1
    partner = lax.rem(pole + half_poles, poles)
    core = lax.rem(space, 2)
    chip = space // 2
    sibling = space + 1 - 2 * core
    has_previous, has_following = space > 0, space < 2 * chips - 1
    steps = (1, -1, 2, -2, 3, -3)

    def has(step):
        return jnp.logical_and(chip + step >= 0, chip + step < chips)

    own = HALO + 2 * core
    own_copies = [
        pltpu.make_async_copy(kappa_ref, stage.at[0], loc.at[0]),
        pltpu.make_async_copy(misfit_ref, stage.at[1], loc.at[1]),
        pltpu.make_async_copy(forward_ref, stage.at[pl.ds(2, 2)], loc.at[2]),
        pltpu.make_async_copy(shift_ref, shift_mem, loc.at[3]),
        pltpu.make_async_copy(weight_ref, weight_mem, loc.at[4]),
        pltpu.make_async_copy(order_ref, order_mem, loc.at[5]),
    ]
    for copy in own_copies:
        copy.start()

    barrier = pltpu.get_barrier_semaphore()

    def greet(p, s):
        pl.semaphore_signal(barrier, inc=1, device_id=(p, s), device_id_type=MESH)

    across = space + 2 * core - 1
    has_across = jnp.logical_and(across >= 0, across < 2 * chips)
    expected = half_poles + has_across.astype(jnp.int32) + late.astype(jnp.int32)
    for step in steps:
        expected = expected + has(step).astype(jnp.int32)

        @pl.when(has(step))
        def _():
            greet(pole, space + 2 * step)

    greet(pole, sibling)

    @pl.when(has_across)
    def _():
        greet(pole, across)

    for d in range(1, half_poles):
        greet(half * half_poles + lax.rem(yy + d, half_poles), space)

    @pl.when(early)
    def _():
        greet(partner, space)

    for step in steps:
        @pl.when(jnp.logical_not(has(step)))
        def _():
            zeros = jnp.zeros((4, 8, 8, NZ), jnp.float32)
            kap[pl.ds(HALO + 4 * step, 4)] = zeros
            res[pl.ds(HALO + 4 * step, 4)] = zeros

    @pl.when(jnp.logical_not(has_previous))
    def _():
        fwd[:, 0] = jnp.zeros((4, 8, 8, NZ), jnp.float32)

    @pl.when(jnp.logical_not(has_following))
    def _():
        fwd[:, 3] = jnp.zeros((4, 8, 8, NZ), jnp.float32)

    stage_far[:, :, TOP:] = jnp.zeros((2, 2, NY - TOP, NZ), jnp.float32)
    lane_in = lax.rem(lax.broadcasted_iota(jnp.int32, (3 * NZ, 2 * NZ), 0), NZ)
    lane_out = lax.broadcasted_iota(jnp.int32, (3 * NZ, 2 * NZ), 1)
    source_lane = jnp.where(lane_out < NZ, lane_out + 1, lane_out - NZ - 1)
    shifts[...] = jnp.where(lane_in == source_lane, 1.0, 0.0).astype(jnp.bfloat16)

    for copy in own_copies:
        copy.wait()
    for n in range(2):
        kap[own + n] = 0.5 * natural(stage, (0, n))
        res[own + n] = natural(stage, (1, n))
        for slot in range(2):
            fwd[slot, 1 + n] = natural(stage, (2 + slot, n))
    pole_here = order_mem[core]
    own_shift = shift_mem[pole_here]
    param[0, 0] = jnp.full((8, NZ), own_shift, jnp.float32)
    param[0, 1] = jnp.full((8, NZ), weight_mem[pole_here], jnp.float32)

    pl.semaphore_wait(barrier, expected)

    def send_token(k):
        for a, step in enumerate((TOKENS[k], -TOKENS[k])):
            @pl.when(has(step))
            def _():
                pl.semaphore_signal(token.at[k, a], inc=1, device_id=(pole, space + 2 * step), device_id_type=MESH)

    def take_token(k):
        for a, step in enumerate((TOKENS[k], -TOKENS[k])):
            @pl.when(has(-step))
            def _():
                pl.semaphore_wait(token.at[k, a], 1)

    send_token(0)

    def remote(src, dst, send, recv, p, s):
        return pltpu.make_async_remote_copy(
            src_ref=src, dst_ref=dst, send_sem=send, recv_sem=recv,
            device_id=(p, s), device_id_type=MESH,
        )

    def block_copy(i, step, target):
        return [
            remote(dest.at[pl.ds(own, 2)], dest.at[pl.ds(own - 4 * step, 2)],
                   near_send.at[a, i], near_recv.at[a, i], pole, target)
            for a, dest in enumerate((kap, res))
        ]

    def outgoing(i, step):
        return block_copy(i, step, space + 2 * step)

    def incoming(i, step):
        return block_copy(i, step, space - 2 * step)

    def passing(i, at):
        return [
            remote(dest.at[pl.ds(at, 2)], dest.at[pl.ds(at, 2)], sib_send.at[a, i], sib_recv.at[a, i],
                   pole, sibling)
            for a, dest in enumerate((kap, res))
        ]

    for i, step in enumerate(steps):
        @pl.when(has(step))
        def _():
            for copy in outgoing(i, step):
                copy.start()

    for copy in passing(6, own):
        copy.start()

    far_copies = [
        remote(param.at[0], param.at[1], far_send.at[0], far_recv.at[0], partner, space),
        remote(stage.at[pl.ds(2, 2), :, pl.ds(0, TOP)], stage_far.at[:, :, pl.ds(0, TOP)],
               far_send.at[1], far_recv.at[1], partner, space),
    ]

    @pl.when(late)
    def _():
        for copy in far_copies:
            copy.start()

    def to_previous(k):
        return remote(fwd.at[pl.ds(2 * k, 2), 1], fwd.at[pl.ds(2 * k, 2), 3],
                      f_send.at[2 * k], f_recv.at[2 * k], pole, space - 1)

    def to_following(k):
        return remote(fwd.at[pl.ds(2 * k, 2), 2], fwd.at[pl.ds(2 * k, 2), 0],
                      f_send.at[2 * k + 1], f_recv.at[2 * k + 1], pole, space + 1)

    def send_forward(k):
        @pl.when(has_previous)
        def _():
            to_previous(k).start()

        @pl.when(has_following)
        def _():
            to_following(k).start()

    def wait_forward(k):
        @pl.when(has_previous)
        def _():
            to_following(k).wait_recv()

        @pl.when(has_following)
        def _():
            to_previous(k).wait_recv()

    def sent_forward(k):
        @pl.when(has_previous)
        def _():
            to_previous(k).wait_send()

        @pl.when(has_following)
        def _():
            to_following(k).wait_send()

    send_forward(0)

    block = (8, 8, NZ)
    row = 8 * lax.broadcasted_iota(jnp.int32, block, 1) + lax.broadcasted_iota(jnp.int32, block, 0)
    col = lax.broadcasted_iota(jnp.int32, block, 2)
    row_first, row_last = row == 0, row == NY - 1
    col_first, col_last = col == 0, col == NZ - 1
    top = row < NY // 2
    col_odd = lax.rem(lax.broadcasted_iota(jnp.int32, (4, 8, NZ), 2), 2) == 1

    def inside(i):
        plane = 4 * chip + i - HALO
        return jnp.logical_and(plane >= 0, plane < 4 * chips)

    def fine_faces(i, odd):
        k = kap[i]
        fx, bx = k + kap[i + 1], k + kap[i - 1]
        py = k + jnp.where(row_last, 0.0, next_row(k))
        qy = jnp.where(row_first, k, previous_row(py))
        pz = k + jnp.where(col_last, 0.0, roll(k, -1, 2))
        qz = jnp.where(col_first, k, roll(pz, 1, 2))
        my, mz = jnp.where(row_last, 0.0, py), jnp.where(col_last, 0.0, pz)
        face_x[i] = fx
        face_y[i] = my
        face_z[i] = mz
        down_z[i] = jnp.where(col_first, 0.0, qz)
        b = (fx + bx) + (py + qy) + (pz + qz)
        base[i] = b
        d = b + own_shift
        g = jnp.where(inside(i), W, 0.0) / d
        diag[i] = d
        gain[i] = g
        z1[i] = g * res[i]
        around = row_pairs(fx if odd else bx), rows_of(qy)[0] + rows_of(py)[1], row_pairs(pz), row_pairs(qz)
        return fx, around, rows_of(my)[1], row_pairs(mz)

    def faces(j):
        i = 2 * j
        _, (bx0, by0, pz0, qz0), fy0, fz0 = fine_faces(i, False)
        fx, (bx1, by1, pz1, qz1), fy1, fz1 = fine_faces(i + 1, True)
        cface_x[j] = pair_sum(fx)
        fy = fy0 + fy1
        cface_y[j] = fy + roll(fy, -1, 2)
        cface_z[j] = roll(fz0 + fz1, -1, 2)
        both = (bx0 + bx1) + (by0 + by1)
        d = both + (qz0 + qz1) + roll(both + (pz0 + pz1), -1, 2)
        cbase[j] = d
        cgain[j] = jnp.where(inside(i), W, 0.0) / (d + 8.0 * own_shift)

    middle = HALO // 2
    other = HALO + 2 * (1 - core)
    for copy in passing(6, other):
        copy.wait_recv()
    for ring in range(3):
        pair = tuple(enumerate(steps))[2 * ring : 2 * ring + 2]
        for i, step in pair:
            @pl.when(has(-step))
            def _():
                for copy in incoming(i, step):
                    copy.wait_recv()
                for copy in passing(i, own - 4 * step):
                    copy.start()
        for i, step in pair:
            @pl.when(has(-step))
            def _():
                for copy in passing(i, other - 4 * step):
                    copy.wait_recv()
        take_token(ring)
        send_token(ring + 1)
        if ring == 0:
            rows = (middle - 1, middle, middle + 1, middle + 2)
        else:
            rows = (middle - 2 * ring - 1, middle - 2 * ring, middle + 2 * ring + 1, middle + 2 * ring + 2)
        for j in rows:
            faces(j)
    face_x[0] = kap[0] + kap[1]
    fine_faces(1, True)
    fine_faces(PLANES - 2, False)

    def off(vm, v, vp, fm, fx, fy):
        total = fx * vp + fm * vm
        return total + (fy * next_row(v) + previous_row(fy * v))

    def lane_rolls(fz, v, by):
        return fz * roll(v, -by, 2) + roll(fz * v, by, 2)

    def fine_lanes(i, v):
        if i % 2:
            return lane_rolls(face_z[i], v, 1)
        after, before = lane_sides(v, shifts[...])
        return face_z[i] * after + down_z[i] * before

    def coarse_lanes(j, v):
        return lane_rolls(cface_z[j], v, 2)

    def sweep(ref, lo, hi, faces_xy, lanes, emit):
        px, py = faces_xy
        vm, v, fm = ref[lo - 1], ref[lo], px[lo - 1]
        for i in range(lo, hi):
            vp, fx = ref[i + 1], px[i]
            emit(i, off(vm, v, vp, fm, fx, py[i]) + lanes(i, v), v)
            vm, v, fm = v, vp, fx

    fine_xy, coarse_xy = (face_x, face_y), (cface_x, cface_y)

    def precondition(source, out, lo, hi):
        first, last = (lo - 1) // 2, hi // 2
        held = []

        def down(i, part_off, v):
            held.append(0.2 * source[i] + part_off)
            if i % 2:
                y1[i // 2] = cgain[i // 2] * pair_sum(held[-2] + held[-1])

        def up(j, part_off, v):
            i = 2 * j
            y2 = 1.2 * v + cgain[j] * part_off
            y2 = jnp.where(col_odd, roll(y2, 1, 2), y2)
            y2 = jnp.stack([y2, y2], axis=1).reshape(block)
            z2[i] = z1[i] + y2
            z2[i + 1] = z1[i + 1] + y2

        def smooth(i, part_off, v):
            out[i] = 0.2 * v + z1[i] + gain[i] * part_off

        sweep(z1, 2 * first - 2, 2 * last + 4, fine_xy, fine_lanes, down)
        sweep(y1, first, last + 1, coarse_xy, coarse_lanes, up)
        sweep(z2, lo, hi, fine_xy, fine_lanes, smooth)

    window = HALO - 1 + 2 * core
    sib_window = HALO + 1 - 2 * core

    def exchange(e):
        return [
            remote(mine.at[e, pl.ds(sib_window, 4)], theirs.at[e], xs_send.at[e, a], xs_recv.at[e, a],
                   pole, sibling)
            for a, (mine, theirs) in enumerate(((u0, sib_u), (ut, sib_t)))
        ]

    sub = lax.broadcasted_iota(jnp.int32, (8, NZ), 0)
    lane = lax.broadcasted_iota(jnp.int32, (8, NZ), 1)
    part[0] = jnp.zeros((8, NZ), jnp.float32)

    def solve(e, carry):
        @pl.when(e == 1)
        def _():
            far_copies[0].wait_recv()
            shift = param[1, 0]
            for i in range(1, PLANES - 1):
                d = base[i] + shift
                g = jnp.where(inside(i), W, 0.0) / d
                diag[i] = d
                gain[i] = g
                z1[i] = g * res[i]
            for j in range(1, PLANES // 2 - 1):
                cgain[j] = jnp.where(inside(2 * j), W, 0.0) / (cbase[j] + 8.0 * shift)

        u, t = u0.at[e], ut.at[e]
        precondition(res, u, HALO - 6, HALO + 10)

        def residual(i, part_off, v):
            value = res[i] - (diag[i] * v - part_off)
            rt[i] = value
            z1[i] = gain[i] * value

        sweep(u, HALO - 5, HALO + 9, fine_xy, fine_lanes, residual)
        precondition(rt, t, HALO - 1, HALO + 5)
        for copy in exchange(e):
            copy.start()
        totals = [jnp.zeros((8, NZ), jnp.float32)] * 4

        def products(i, part_off, v):
            image = diag[i] * v - part_off
            un, rn, tn = u[i], res[i], rt[i]
            for k, product in enumerate((un * rn, un * tn, tn * v, v * image)):
                totals[k] = totals[k] + jnp.sum(product, axis=0)

        sweep(t, HALO, HALO + 4, fine_xy, fine_lanes, products)
        tile = part[0]
        for k, total in enumerate(totals):
            tile = jnp.where(sub == 4 * e + k, jnp.sum(total, axis=0, keepdims=True), tile)
        part[0] = tile
        return carry

    lax.fori_loop(0, 2 - half, solve, 0)
    take_token(len(TOKENS) - 1)

    def reduce_start(d, carry):
        remote(part.at[0], part.at[d], ar_send, ar_recv, pole, lax.rem(space + 2 * d, 2 * chips)).start()
        return carry

    lax.fori_loop(1, chips, reduce_start, 0)

    @pl.when(early)
    def _():
        far_copies[1].wait_recv()
        for slot in range(2):
            for n in range(2):
                fwd[2 + slot, 1 + n] = natural(stage_far, (slot, n))
        send_forward(1)

    def everyone(sem):
        return pltpu.make_async_copy(part.at[pl.ds(1, chips - 1)], part.at[pl.ds(1, chips - 1)], sem)

    everyone(ar_recv).wait()
    total = jnp.sum(jnp.sum(part[...], axis=0), axis=1, keepdims=True)
    factors = []
    for e in range(2):
        g0, d0, e1, m0 = (total[4 * e + k : 4 * e + k + 1] for k in range(4))
        weight = param[e, 1][0:1, 0:1]
        c0 = g0 - d0
        eta = d0 / c0
        a0 = 1.0 + eta
        t = d0 - e1
        k = c0 - t
        g1 = e1 - 2.0 * eta * t + eta * eta * k
        b = g1 / g0
        s11 = m0 - 2.0 * eta * (t - m0) + eta * eta * (k - t + m0)
        c1 = s11 + 2.0 * b * (t - eta * k) + b * b * c0
        a1 = g1 / c1
        factors += [weight * (a0 + a1 * (b - eta)), weight * (a1 * a0)]
    tile = jnp.broadcast_to(factors[0], (8, NZ))
    for k in range(1, 4):
        tile = jnp.where(lane == k, factors[k], tile)
    sums[...] = tile
    scalars = remote(sums, swap, sw_send, sw_recv, pole, sibling)
    scalars.start()

    def combine(source_u, source_t, at, slot, one, two):
        for n in range(4):
            xout[slot, n] = one * source_u[at + n] + two * source_t[at + n]

    combine(u0.at[0], ut.at[0], window, core, factors[0], factors[1])

    @pl.when(early)
    def _():
        combine(u0.at[1], ut.at[1], window, 2 + core, sums[0:1, 2:3], sums[0:1, 3:4])

    for copy in exchange(0):
        copy.wait_recv()
    scalars.wait_recv()
    combine(sib_u.at[0], sib_t.at[0], 0, 1 - core, swap[0:1, 0:1], swap[0:1, 1:2])

    @pl.when(early)
    def _():
        for copy in exchange(1):
            copy.wait_recv()
        combine(sib_u.at[1], sib_t.at[1], 0, 3 - core, swap[0:1, 2:3], swap[0:1, 3:4])
        wait_forward(1)

    wait_forward(0)

    def ahead_row(v):
        return jnp.where(row_last, 0.0, next_row(v))

    def ahead_col(v):
        return jnp.where(col_last, 0.0, roll(v, -1, 2))

    def slot_term(slot, n):
        x, f = xout[slot, n], fwd[slot, n]
        total = (x - xout[slot, n + 1]) * (f - fwd[slot, n + 1])
        total = total + (x - xout[slot, n - 1]) * (f - fwd[slot, n - 1])
        product = x * f
        ahead = (x - ahead_row(x)) * (f - ahead_row(f))
        total = total + ahead + jnp.where(row_first, product, previous_row(ahead))
        ahead = (x - ahead_col(x)) * (f - ahead_col(f))
        return total + ahead + jnp.where(col_first, product, roll(ahead, 1, 2))

    for n in (1, 2):
        mine = slot_term(0, n) + slot_term(1, n)
        extra = lax.fori_loop(
            2, 4 - 2 * half, lambda slot, acc: acc + slot_term(slot, n), jnp.zeros(block, jnp.float32)
        )
        put_natural(term, (n - 1,), -0.5 * (mine + jnp.where(top, extra, 0.0)))

    def rows_for(q):
        return pl.ds(pl.multiple_of(8 * q, 8), 8)

    def spread(d, upper):
        q = lax.rem(yy + d, half_poles)
        k = 0 if upper else 1
        return remote(term.at[:, rows_for(q if upper else q + half_poles), :], pieces.at[k, d],
                      rs_send.at[k, d], rs_recv.at[k, d], half * half_poles + q, space)

    @pl.when(early)
    def _():
        for d in range(1, half_poles):
            spread(d, True).start()

    for d in range(1, half_poles):
        spread(d, False).start()

    for slot in range(2):
        for n in range(2):
            put_natural(xnat, (slot, n), xout[slot, 1 + n])
    adjoint_out = pltpu.make_async_copy(xnat, adjoint_ref, loc.at[0])
    adjoint_out.start()

    share = remote(gfar, gnear, far_send.at[2], far_recv.at[2], partner, space)
    gradient_out = pltpu.make_async_copy(gout, gradient_ref, loc.at[1])

    def collect(k, q):
        total = term[:, rows_for(q), :]
        for d in range(1, half_poles):
            spread(d, k == 0).wait_recv()
            total = total + pieces[k, d]
        return total

    @pl.when(early)
    def _():
        gout[...] = collect(0, yy)
        gradient_out.start()
        gfar[...] = collect(1, yy + half_poles)
        share.start()

    @pl.when(late)
    def _():
        total = collect(1, yy + half_poles)
        share.wait_recv()
        gout[...] = total + gnear[...]
        gradient_out.start()

    for i, step in enumerate(steps):
        @pl.when(has(step))
        def _():
            for copy in outgoing(i, step):
                copy.wait_send()

        @pl.when(has(-step))
        def _():
            for copy in passing(i, own - 4 * step):
                copy.wait_send()
    for copy in passing(6, own):
        copy.wait_send()
    sent_forward(0)
    for copy in exchange(0):
        copy.wait_send()
    everyone(ar_send).wait()
    scalars.wait_send()
    for d in range(1, half_poles):
        spread(d, False).wait_send()

    @pl.when(early)
    def _():
        sent_forward(1)
        for copy in exchange(1):
            copy.wait_send()
        for d in range(1, half_poles):
            spread(d, True).wait_send()
        share.wait_send()

    @pl.when(late)
    def _():
        for copy in far_copies:
            copy.wait_send()

    adjoint_out.wait()
    gradient_out.wait()


def solution(mesh):
    chips, poles = mesh.shape["space"] // 2, mesh.shape["pole"]
    f32 = jnp.float32

    def per_device(conductivity, misfit, forward_states, pole_shifts, pole_weights, pole_order):
        hbm = pl.BlockSpec(memory_space=pltpu.HBM)
        fine = pltpu.VMEM((PLANES, 8, 8, NZ), f32)
        coarse = pltpu.VMEM((PLANES // 2, 4, 8, NZ), f32)
        pair = pltpu.VMEM((2, PLANES, 8, 8, NZ), f32)
        windows = pltpu.VMEM((2, 4, 8, 8, NZ), f32)
        slots = pltpu.VMEM((4, 4, 8, 8, NZ), f32)
        tile = pltpu.VMEM((8, NZ), f32)
        piece = (2, NY // poles, NZ)
        dma = pltpu.SemaphoreType.DMA
        return pl.pallas_call(
            functools.partial(kernel, chips, poles),
            out_shape=(
                jax.ShapeDtypeStruct(forward_states.shape, f32),
                jax.ShapeDtypeStruct(piece, f32),
            ),
            in_specs=[hbm] * 6,
            out_specs=(hbm, hbm),
            scratch_shapes=[
                pltpu.SMEM(pole_shifts.shape, f32), pltpu.SMEM(pole_weights.shape, f32),
                pltpu.SMEM(pole_order.shape, jnp.int32),
            ] + [fine] * 12 + [coarse] * 6 + [
                pair, pair, windows, windows, slots, slots,
                pltpu.VMEM((4, 2, NY, NZ), f32), pltpu.VMEM((2, 2, NY, NZ), f32), pltpu.VMEM((2, 2, NY, NZ), f32),
                pltpu.VMEM((2, NY, NZ), f32), pltpu.VMEM((2, 2, 8, NZ), f32),
                pltpu.VMEM((chips, 8, NZ), f32), tile, tile,
                pltpu.VMEM((2, poles // 2, *piece), f32), pltpu.VMEM(piece, f32), pltpu.VMEM(piece, f32),
                pltpu.VMEM(piece, f32), pltpu.VMEM((3 * NZ, 2 * NZ), jnp.bfloat16),
                dma((6,)), dma((2, 6)), dma((2, 6)), dma((2, 7)), dma((2, 7)), dma((4,)), dma((4,)),
                dma, dma, dma, dma, dma((2, 2)), dma((2, 2)),
                dma((2, poles // 2)), dma((2, poles // 2)), dma((3,)), dma((3,)),
                pltpu.SemaphoreType.REGULAR((len(TOKENS), 2)),
            ],
            compiler_params=pltpu.CompilerParams(
                collective_id=0, has_side_effects=True, vmem_limit_bytes=64 << 20
            ),
            name="adjoint_gradient",
        )(pole_shifts, pole_weights, pole_order, conductivity, misfit, forward_states)

    in_specs = (
        P("space", None, None), P("space", None, None), P("pole", "space", None, None),
        P(), P(), P("pole"),
    )
    out_specs = (P("pole", "space", None, None), P("space", "pole", None))
    return jax.shard_map(per_device, mesh=mesh, in_specs=in_specs, out_specs=out_specs, check_vma=False)
```

time: 59.2 us -> 57.7 us (0.975)
  Pallas kernels: 56.1 us -> 54.7 us
    pallas_call x1, Pallas kernels: 56.1 us -> 54.7 us  [per_device(): pl.pallas_call(functools.partial(kernel, chips, poles), out_shape=(jax.Sh...]
where the time goes in v3:
time: 57.7 us; the launch traced here: 57.6 us
  Pallas kernels  54.7 us (95%)
  local copies, waits for them, and re-layouts  2.18 us (4%)
  between operations  0.65 us (1%)
    pallas_call x1, Pallas kernels, per_device(): pl.pallas_call(functools.partial(kernel, chips, poles), out_shape=(jax.Sh...  54.7 us
    unnamed x4, local copies, waits for them, and re-layouts  2.18 us

profile of v3, /device:TPU:1, one launch (start us, length us, event | category | flops | bytes accessed | tf_op | source)
XLA Modules:
  0.0 57.6 jit_solution(12972470717123984332)
XLA Ops:
  0.6 54.7 %adjoint_gradient.1 = (f32[2,2,64,128]{3,2,1,0:T(8,128)}, f32[2,8,128]{2,1,0:T(8,128)}) custom-call(f32[16]{0:T(128)} %shift_ref.1, f32[16]{0:T(128)} %weight_ref.1, s32[2]{0:T(128)} %order_ref.1, f32[2,64,128]{2,1,0:T(8,128)} %kappa_ref.1, f32[2,64,128]{2,1,0:T(8,128)} %misfit_ref.1, f32[2,2,64,128]{3,2,1,0:T(8,128)} %forward_ref.1), custom_call_target="tpu_custom_call" | custom-call | tf_op jit(solution)/shard_map/adjoint_gradient/pallas_call | solution.py:635
  55.4 0.0 copy-start
  55.4 1.6 %copy.10 = f32[2,2,64,128]{3,2,1,0:T(8,128)} copy(f32[2,2,64,128]{3,2,1,0:T(8,128)} %get-tuple-element.4) | data formatting | bytes 262144
  57.0 0.0 copy-done
  57.0 0.6 %copy.11 = f32[2,8,128]{2,1,0:T(8,128)} copy(f32[2,8,128]{2,1,0:T(8,128)S(1)} %copy-done) | data formatting | bytes 16384
Async XLA Ops:
  55.4 1.6 %copy-start = (f32[2,8,128]{2,1,0:T(8,128)S(1)}, f32[2,8,128]{2,1,0:T(8,128)}, u32[]{:S(2)}) copy-start(f32[2,8,128]{2,1,0:T(8,128)} %get-tuple-element.5) | copy-start | bytes 24580

commit v4 on v3

--- a/solution.py
+++ b/solution.py
@@ -69,9 +69,9 @@
     shift_mem, weight_mem, order_mem,
     kap, res, face_x, face_y, face_z, down_z, base, diag, gain, z1, z2, rt,
     cface_x, cface_y, cface_z, cbase, cgain, y1, u0, ut,
-    sib_u, sib_t, fwd, xout, stage, stage_far, xnat, term, param, part, sums, swap, pieces, gout, gfar, gnear, shifts,
+    sib_u, sib_t, fwd, parts, stage, stage_far, xnat, term, param, part, sums, swap, pieces, gout, gfar, gnear, shifts,
     loc, near_send, near_recv, sib_send, sib_recv, f_send, f_recv, ar_send, ar_recv, sw_send, sw_recv,
-    xs_send, xs_recv, rs_send, rs_recv, far_send, far_recv, token,
+    xs_send, xs_recv, rs_send, rs_recv, far_send, far_recv, y_send, y_recv, token,
 ):
     half_poles = poles // 2
     pole = lax.axis_index("pole")
@@ -183,11 +183,23 @@
             device_id=(p, s), device_id_type=MESH,
         )
 
+    part_rows = 8 // half_poles
+    my_part = pl.ds(part_rows * yy, part_rows)
+
     def block_copy(i, step, target):
+        share = (my_part,) if abs(step) >= 2 else ()
         return [
-            remote(dest.at[pl.ds(own, 2)], dest.at[pl.ds(own - 4 * step, 2)],
+            remote(dest.at[(pl.ds(own, 2), *share)], dest.at[(pl.ds(own - 4 * step, 2), *share)],
                    near_send.at[a, i], near_recv.at[a, i], pole, target)
             for a, dest in enumerate((kap, res))
+        ]
+
+    def share_copy(i, step):
+        at = (pl.ds(own - 4 * step, 2), my_part)
+        return [
+            remote(dest.at[at], dest.at[at], y_send.at[a, i - 2, d], y_recv.at[a, i - 2, d],
+                   half * half_poles + lax.rem(yy + d, half_poles), space)
+            for a, dest in enumerate((kap, res)) for d in range(1, half_poles)
         ]
 
     def outgoing(i, step):
@@ -203,10 +215,10 @@
             for a, dest in enumerate((kap, res))
         ]
 
-    for i, step in enumerate(steps):
-        @pl.when(has(step))
-        def _():
-            for copy in outgoing(i, step):
+    for i in (2, 3, 4, 5, 0, 1):
+        @pl.when(has(steps[i]))
+        def _():
+            for copy in outgoing(i, steps[i]):
                 copy.start()
 
     for copy in passing(6, own):
@@ -311,12 +323,19 @@
     other = HALO + 2 * (1 - core)
     for copy in passing(6, other):
         copy.wait_recv()
+    for i in (2, 3, 4, 5):
+        @pl.when(has(-steps[i]))
+        def _():
+            for copy in incoming(i, steps[i]):
+                copy.wait_recv()
+            for copy in share_copy(i, steps[i]):
+                copy.start()
     for ring in range(3):
         pair = tuple(enumerate(steps))[2 * ring : 2 * ring + 2]
         for i, step in pair:
             @pl.when(has(-step))
             def _():
-                for copy in incoming(i, step):
+                for copy in share_copy(i, step) if ring else incoming(i, step):
                     copy.wait_recv()
                 for copy in passing(i, own - 4 * step):
                     copy.start()
@@ -451,6 +470,33 @@
 
     lax.fori_loop(1, chips, reduce_start, 0)
 
+    def ahead_row(v):
+        return jnp.where(row_last, 0.0, next_row(v))
+
+    def ahead_col(v):
+        return jnp.where(col_last, 0.0, roll(v, -1, 2))
+
+    def slot_terms(e, who, fields, at):
+        slot = 2 * e + (core if who == 0 else 1 - core)
+        for n in (1, 2):
+            f = fwd[slot, n]
+            f_next, f_last = f - fwd[slot, n + 1], f - fwd[slot, n - 1]
+            f_row, f_col = f - ahead_row(f), f - ahead_col(f)
+            for k, ref in enumerate(fields):
+                x = ref[at + n]
+                total = (x - ref[at + n + 1]) * f_next + (x - ref[at + n - 1]) * f_last
+                product = x * f
+                ahead = (x - ahead_row(x)) * f_row
+                total = total + ahead + jnp.where(row_first, product, previous_row(ahead))
+                ahead = (x - ahead_col(x)) * f_col
+                parts[e, who, k, n - 1] = total + ahead + jnp.where(col_first, product, roll(ahead, 1, 2))
+
+    for copy in exchange(0):
+        copy.wait_recv()
+    wait_forward(0)
+    slot_terms(0, 0, (u0.at[0], ut.at[0]), window)
+    slot_terms(0, 1, (sib_u.at[0], sib_t.at[0]), 0)
+
     @pl.when(early)
     def _():
         far_copies[1].wait_recv()
@@ -458,6 +504,11 @@
             for n in range(2):
                 fwd[2 + slot, 1 + n] = natural(stage_far, (slot, n))
         send_forward(1)
+        for copy in exchange(1):
+            copy.wait_recv()
+        wait_forward(1)
+        slot_terms(1, 0, (u0.at[1], ut.at[1]), window)
+        slot_terms(1, 1, (sib_u.at[1], sib_t.at[1]), 0)
 
     def everyone(sem):
         return pltpu.make_async_copy(part.at[pl.ds(1, chips - 1)], part.at[pl.ds(1, chips - 1)], sem)
@@ -485,53 +536,22 @@
     sums[...] = tile
     scalars = remote(sums, swap, sw_send, sw_recv, pole, sibling)
     scalars.start()
-
-    def combine(source_u, source_t, at, slot, one, two):
-        for n in range(4):
-            xout[slot, n] = one * source_u[at + n] + two * source_t[at + n]
-
-    combine(u0.at[0], ut.at[0], window, core, factors[0], factors[1])
+    scalars.wait_recv()
+
+    def weighted(e, n):
+        factor = [ref[0:1, 2 * e + k : 2 * e + k + 1] for ref in (sums, swap) for k in range(2)]
+        own_part = factor[0] * parts[e, 0, 0, n] + factor[1] * parts[e, 0, 1, n]
+        return own_part + (factor[2] * parts[e, 1, 0, n] + factor[3] * parts[e, 1, 1, n])
+
+    @pl.when(late)
+    def _():
+        for n in range(2):
+            put_natural(term, (n,), -0.5 * weighted(0, n))
 
     @pl.when(early)
     def _():
-        combine(u0.at[1], ut.at[1], window, 2 + core, sums[0:1, 2:3], sums[0:1, 3:4])
-
-    for copy in exchange(0):
-        copy.wait_recv()
-    scalars.wait_recv()
-    combine(sib_u.at[0], sib_t.at[0], 0, 1 - core, swap[0:1, 0:1], swap[0:1, 1:2])
-
-    @pl.when(early)
-    def _():
-        for copy in exchange(1):
-            copy.wait_recv()
-        combine(sib_u.at[1], sib_t.at[1], 0, 3 - core, swap[0:1, 2:3], swap[0:1, 3:4])
-        wait_forward(1)
-
-    wait_forward(0)
-
-    def ahead_row(v):
-        return jnp.where(row_last, 0.0, next_row(v))
-
-    def ahead_col(v):
-        return jnp.where(col_last, 0.0, roll(v, -1, 2))
-
-    def slot_term(slot, n):
-        x, f = xout[slot, n], fwd[slot, n]
-        total = (x - xout[slot, n + 1]) * (f - fwd[slot, n + 1])
-        total = total + (x - xout[slot, n - 1]) * (f - fwd[slot, n - 1])
-        product = x * f
-        ahead = (x - ahead_row(x)) * (f - ahead_row(f))
-        total = total + ahead + jnp.where(row_first, product, previous_row(ahead))
-        ahead = (x - ahead_col(x)) * (f - ahead_col(f))
-        return total + ahead + jnp.where(col_first, product, roll(ahead, 1, 2))
-
-    for n in (1, 2):
-        mine = slot_term(0, n) + slot_term(1, n)
-        extra = lax.fori_loop(
-            2, 4 - 2 * half, lambda slot, acc: acc + slot_term(slot, n), jnp.zeros(block, jnp.float32)
-        )
-        put_natural(term, (n - 1,), -0.5 * (mine + jnp.where(top, extra, 0.0)))
+        for n in range(2):
+            put_natural(term, (n,), -0.5 * (weighted(0, n) + jnp.where(top, weighted(1, n), 0.0)))
 
     def rows_for(q):
         return pl.ds(pl.multiple_of(8 * q, 8), 8)
@@ -550,9 +570,10 @@
     for d in range(1, half_poles):
         spread(d, False).start()
 
-    for slot in range(2):
+    for ref, fields, at, slot in ((sums, (u0.at[0], ut.at[0]), window, core), (swap, (sib_u.at[0], sib_t.at[0]), 0, 1 - core)):
         for n in range(2):
-            put_natural(xnat, (slot, n), xout[slot, 1 + n])
+            value = ref[0:1, 0:1] * fields[0][at + 1 + n] + ref[0:1, 1:2] * fields[1][at + 1 + n]
+            put_natural(xnat, (slot, n), value)
     adjoint_out = pltpu.make_async_copy(xnat, adjoint_ref, loc.at[0])
     adjoint_out.start()
 
@@ -590,6 +611,9 @@
         def _():
             for copy in passing(i, own - 4 * step):
                 copy.wait_send()
+            if abs(step) >= 2:
+                for copy in share_copy(i, step):
+                    copy.wait_send()
     for copy in passing(6, own):
         copy.wait_send()
     sent_forward(0)
@@ -644,7 +668,7 @@
                 pltpu.SMEM(pole_shifts.shape, f32), pltpu.SMEM(pole_weights.shape, f32),
                 pltpu.SMEM(pole_order.shape, jnp.int32),
             ] + [fine] * 12 + [coarse] * 6 + [
-                pair, pair, windows, windows, slots, slots,
+                pair, pair, windows, windows, slots, pltpu.VMEM((2, 2, 2, 2, 8, 8, NZ), f32),
                 pltpu.VMEM((4, 2, NY, NZ), f32), pltpu.VMEM((2, 2, NY, NZ), f32), pltpu.VMEM((2, 2, NY, NZ), f32),
                 pltpu.VMEM((2, NY, NZ), f32), pltpu.VMEM((2, 2, 8, NZ), f32),
                 pltpu.VMEM((chips, 8, NZ), f32), tile, tile,
@@ -653,7 +677,7 @@
                 dma((6,)), dma((2, 6)), dma((2, 6)), dma((2, 7)), dma((2, 7)), dma((4,)), dma((4,)),
                 dma, dma, dma, dma, dma((2, 2)), dma((2, 2)),
                 dma((2, poles // 2)), dma((2, poles // 2)), dma((3,)), dma((3,)),
-                pltpu.SemaphoreType.REGULAR((len(TOKENS), 2)),
+                dma((2, 4, poles // 2)), dma((2, 4, poles // 2)), pltpu.SemaphoreType.REGULAR((len(TOKENS), 2)),
             ],
             compiler_params=pltpu.CompilerParams(
                 collective_id=0, has_side_effects=True, vmem_limit_bytes=64 << 20

time: 57.7 us -> 51.8 us (0.90)
  Pallas kernels: 54.7 us -> 48.8 us
    pallas_call x1, Pallas kernels: 54.7 us -> 48.8 us  [per_device(): pl.pallas_call(functools.partial(kernel, chips, poles), out_shape=(jax.Sh...]
where the time goes in v4:
time: 51.8 us; the launch traced here: 51.6 us
  Pallas kernels  48.8 us (94%)
  local copies, waits for them, and re-layouts  2.18 us (4%)
  between operations  0.65 us (1%)
    pallas_call x1, Pallas kernels, per_device(): pl.pallas_call(functools.partial(kernel, chips, poles), out_shape=(jax.Sh...  48.8 us
    unnamed x4, local copies, waits for them, and re-layouts  2.18 us

profile of v4, /device:TPU:1, one launch (start us, length us, event | category | flops | bytes accessed | tf_op | source)
XLA Modules:
  0.0 51.6 jit_solution(6831332914868221899)
XLA Ops:
  0.6 48.8 %adjoint_gradient.1 = (f32[2,2,64,128]{3,2,1,0:T(8,128)}, f32[2,8,128]{2,1,0:T(8,128)}) custom-call(f32[16]{0:T(128)} %shift_ref.1, f32[16]{0:T(128)} %weight_ref.1, s32[2]{0:T(128)} %order_ref.1, f32[2,64,128]{2,1,0:T(8,128)} %kappa_ref.1, f32[2,64,128]{2,1,0:T(8,128)} %misfit_ref.1, f32[2,2,64,128]{3,2,1,0:T(8,128)} %forward_ref.1), custom_call_target="tpu_custom_call" | custom-call | tf_op jit(solution)/shard_map/adjoint_gradient/pallas_call | solution.py:659
  49.4 0.0 copy-start
  49.4 1.6 %copy.10 = f32[2,2,64,128]{3,2,1,0:T(8,128)} copy(f32[2,2,64,128]{3,2,1,0:T(8,128)} %get-tuple-element.4) | data formatting | bytes 262144
  51.0 0.0 copy-done
  51.0 0.6 %copy.11 = f32[2,8,128]{2,1,0:T(8,128)} copy(f32[2,8,128]{2,1,0:T(8,128)S(1)} %copy-done) | data formatting | bytes 16384
Async XLA Ops:
  49.4 1.6 %copy-start = (f32[2,8,128]{2,1,0:T(8,128)S(1)}, f32[2,8,128]{2,1,0:T(8,128)}, u32[]{:S(2)}) copy-start(f32[2,8,128]{2,1,0:T(8,128)} %get-tuple-element.5) | copy-start | bytes 24580

commit v5 on v4

--- a/solution.py
+++ b/solution.py
@@ -67,13 +67,14 @@
     shift_ref, weight_ref, order_ref, kappa_ref, misfit_ref, forward_ref,
     adjoint_ref, gradient_ref,
     shift_mem, weight_mem, order_mem,
-    kap, res, face_x, face_y, face_z, down_z, base, diag, gain, z1, z2, rt,
+    both_fields, face_x, face_y, face_z, down_z, base, diag, gain, z1, z2, rt,
     cface_x, cface_y, cface_z, cbase, cgain, y1, u0, ut,
-    sib_u, sib_t, fwd, parts, stage, stage_far, xnat, term, param, part, sums, swap, pieces, gout, gfar, gnear, shifts,
+    sib_u, sib_t, fwd, parts, stage, stage_far, term, param, part, sums, swap, pieces, gfar, gnear, shifts,
     loc, near_send, near_recv, sib_send, sib_recv, f_send, f_recv, ar_send, ar_recv, sw_send, sw_recv,
     xs_send, xs_recv, rs_send, rs_recv, far_send, far_recv, y_send, y_recv, token,
 ):
     half_poles = poles // 2
+    kap, res = both_fields.at[0], both_fields.at[1]
     pole = lax.axis_index("pole")
     space = lax.axis_index("space")
     half, yy = pole // half_poles, lax.rem(pole, half_poles)
@@ -189,17 +190,17 @@
     def block_copy(i, step, target):
         share = (my_part,) if abs(step) >= 2 else ()
         return [
-            remote(dest.at[(pl.ds(own, 2), *share)], dest.at[(pl.ds(own - 4 * step, 2), *share)],
-                   near_send.at[a, i], near_recv.at[a, i], pole, target)
-            for a, dest in enumerate((kap, res))
+            remote(both_fields.at[(slice(None), pl.ds(own, 2), *share)],
+                   both_fields.at[(slice(None), pl.ds(own - 4 * step, 2), *share)],
+                   near_send.at[i], near_recv.at[i], pole, target)
         ]
 
     def share_copy(i, step):
-        at = (pl.ds(own - 4 * step, 2), my_part)
+        block = both_fields.at[:, pl.ds(own - 4 * step, 2), my_part]
         return [
-            remote(dest.at[at], dest.at[at], y_send.at[a, i - 2, d], y_recv.at[a, i - 2, d],
+            remote(block, block, y_send.at[i - 2, d], y_recv.at[i - 2, d],
                    half * half_poles + lax.rem(yy + d, half_poles), space)
-            for a, dest in enumerate((kap, res)) for d in range(1, half_poles)
+            for d in range(1, half_poles)
         ]
 
     def outgoing(i, step):
@@ -209,11 +210,8 @@
         return block_copy(i, step, space - 2 * step)
 
     def passing(i, at):
-        return [
-            remote(dest.at[pl.ds(at, 2)], dest.at[pl.ds(at, 2)], sib_send.at[a, i], sib_recv.at[a, i],
-                   pole, sibling)
-            for a, dest in enumerate((kap, res))
-        ]
+        block = both_fields.at[:, pl.ds(at, 2)]
+        return [remote(block, block, sib_send.at[i], sib_recv.at[i], pole, sibling)]
 
     for i in (2, 3, 4, 5, 0, 1):
         @pl.when(has(steps[i]))
@@ -573,12 +571,9 @@
     for ref, fields, at, slot in ((sums, (u0.at[0], ut.at[0]), window, core), (swap, (sib_u.at[0], sib_t.at[0]), 0, 1 - core)):
         for n in range(2):
             value = ref[0:1, 0:1] * fields[0][at + 1 + n] + ref[0:1, 1:2] * fields[1][at + 1 + n]
-            put_natural(xnat, (slot, n), value)
-    adjoint_out = pltpu.make_async_copy(xnat, adjoint_ref, loc.at[0])
-    adjoint_out.start()
+            put_natural(adjoint_ref, (slot, n), value)
 
     share = remote(gfar, gnear, far_send.at[2], far_recv.at[2], partner, space)
-    gradient_out = pltpu.make_async_copy(gout, gradient_ref, loc.at[1])
 
     def collect(k, q):
         total = term[:, rows_for(q), :]
@@ -589,8 +584,7 @@
 
     @pl.when(early)
     def _():
-        gout[...] = collect(0, yy)
-        gradient_out.start()
+        gradient_ref[...] = collect(0, yy)
         gfar[...] = collect(1, yy + half_poles)
         share.start()
 
@@ -598,8 +592,7 @@
     def _():
         total = collect(1, yy + half_poles)
         share.wait_recv()
-        gout[...] = total + gnear[...]
-        gradient_out.start()
+        gradient_ref[...] = total + gnear[...]
 
     for i, step in enumerate(steps):
         @pl.when(has(step))
@@ -638,16 +631,13 @@
         for copy in far_copies:
             copy.wait_send()
 
-    adjoint_out.wait()
-    gradient_out.wait()
-
 
 def solution(mesh):
     chips, poles = mesh.shape["space"] // 2, mesh.shape["pole"]
     f32 = jnp.float32
 
     def per_device(conductivity, misfit, forward_states, pole_shifts, pole_weights, pole_order):
-        hbm = pl.BlockSpec(memory_space=pltpu.HBM)
+        hbm, vmem = pl.BlockSpec(memory_space=pltpu.HBM), pl.BlockSpec(memory_space=pltpu.VMEM)
         fine = pltpu.VMEM((PLANES, 8, 8, NZ), f32)
         coarse = pltpu.VMEM((PLANES // 2, 4, 8, NZ), f32)
         pair = pltpu.VMEM((2, PLANES, 8, 8, NZ), f32)
@@ -659,28 +649,28 @@
         return pl.pallas_call(
             functools.partial(kernel, chips, poles),
             out_shape=(
-                jax.ShapeDtypeStruct(forward_states.shape, f32),
-                jax.ShapeDtypeStruct(piece, f32),
+                pltpu.VMEM(forward_states.shape, f32),
+                pltpu.VMEM(piece, f32),
             ),
             in_specs=[hbm] * 6,
-            out_specs=(hbm, hbm),
+            out_specs=(vmem, vmem),
             scratch_shapes=[
                 pltpu.SMEM(pole_shifts.shape, f32), pltpu.SMEM(pole_weights.shape, f32),
                 pltpu.SMEM(pole_order.shape, jnp.int32),
-            ] + [fine] * 12 + [coarse] * 6 + [
+            ] + [pltpu.VMEM((2, PLANES, 8, 8, NZ), f32)] + [fine] * 10 + [coarse] * 6 + [
                 pair, pair, windows, windows, slots, pltpu.VMEM((2, 2, 2, 2, 8, 8, NZ), f32),
-                pltpu.VMEM((4, 2, NY, NZ), f32), pltpu.VMEM((2, 2, NY, NZ), f32), pltpu.VMEM((2, 2, NY, NZ), f32),
+                pltpu.VMEM((4, 2, NY, NZ), f32), pltpu.VMEM((2, 2, NY, NZ), f32),
                 pltpu.VMEM((2, NY, NZ), f32), pltpu.VMEM((2, 2, 8, NZ), f32),
                 pltpu.VMEM((chips, 8, NZ), f32), tile, tile,
                 pltpu.VMEM((2, poles // 2, *piece), f32), pltpu.VMEM(piece, f32), pltpu.VMEM(piece, f32),
-                pltpu.VMEM(piece, f32), pltpu.VMEM((3 * NZ, 2 * NZ), jnp.bfloat16),
-                dma((6,)), dma((2, 6)), dma((2, 6)), dma((2, 7)), dma((2, 7)), dma((4,)), dma((4,)),
+                pltpu.VMEM((3 * NZ, 2 * NZ), jnp.bfloat16),
+                dma((6,)), dma((6,)), dma((6,)), dma((7,)), dma((7,)), dma((4,)), dma((4,)),
                 dma, dma, dma, dma, dma((2, 2)), dma((2, 2)),
                 dma((2, poles // 2)), dma((2, poles // 2)), dma((3,)), dma((3,)),
-                dma((2, 4, poles // 2)), dma((2, 4, poles // 2)), pltpu.SemaphoreType.REGULAR((len(TOKENS), 2)),
+                dma((4, poles // 2)), dma((4, poles // 2)), pltpu.SemaphoreType.REGULAR((len(TOKENS), 2)),
             ],
             compiler_params=pltpu.CompilerParams(
-                collective_id=0, has_side_effects=True, vmem_limit_bytes=64 << 20
+                collective_id=0, has_side_effects=True, vmem_limit_bytes=62 << 20
             ),
             name="adjoint_gradient",
         )(pole_shifts, pole_weights, pole_order, conductivity, misfit, forward_states)

time: 51.8 us -> 50.3 us (0.971)
  local copies, waits for them, and re-layouts: 2.18 us -> 1.26 us
    unnamed x4 -> x2, local copies, waits for them, and re-layouts: 2.18 us -> 1.26 us
where the time goes in v5:
time: 50.3 us; the launch traced here: 50.2 us
  Pallas kernels  48.3 us (96%)
  local copies, waits for them, and re-layouts  1.26 us (3%)
  between operations  0.64 us (1%)
    pallas_call x1, Pallas kernels, per_device(): pl.pallas_call(functools.partial(kernel, chips, poles), out_shape=(pltpu....  48.3 us
    unnamed x2, local copies, waits for them, and re-layouts  1.26 us

profile of v5, /device:TPU:1, one launch (start us, length us, event | category | flops | bytes accessed | tf_op | source)
XLA Modules:
  0.0 50.2 jit_solution(13173758222417561198)
XLA Ops:
  0.6 48.3 %adjoint_gradient.1 = (f32[2,2,64,128]{3,2,1,0:T(8,128)S(1)}, f32[2,8,128]{2,1,0:T(8,128)S(1)}) custom-call(f32[16]{0:T(128)} %shift_ref.1, f32[16]{0:T(128)} %weight_ref.1, s32[2]{0:T(128)} %order_ref.1, f32[2,64,128]{2,1,0:T(8,128)} %kappa_ref.1, f32[2,64,128]{2,1,0:T(8,128)} %misfit_ref.1, f32[2,2,64,128]{3,2,1,0:T(8,128)} %forward_ref.1), custom_call_target="tpu_custom_call" | custom-call | tf_op jit(solution)/shard_map/adjoint_gradient/pallas_call | solution.py:649
  48.9 0.7 %copy.10 = f32[2,2,64,128]{3,2,1,0:T(8,128)} copy(f32[2,2,64,128]{3,2,1,0:T(8,128)S(1)} %get-tuple-element.2) | data formatting | bytes 262144
  49.6 0.6 %copy.11 = f32[2,8,128]{2,1,0:T(8,128)} copy(f32[2,8,128]{2,1,0:T(8,128)S(1)} %get-tuple-element.3) | data formatting | bytes 16384

commit v6 on v5

--- a/solution.py
+++ b/solution.py
@@ -129,27 +129,6 @@
     def _():
         greet(partner, space)
 
-    for step in steps:
-        @pl.when(jnp.logical_not(has(step)))
-        def _():
-            zeros = jnp.zeros((4, 8, 8, NZ), jnp.float32)
-            kap[pl.ds(HALO + 4 * step, 4)] = zeros
-            res[pl.ds(HALO + 4 * step, 4)] = zeros
-
-    @pl.when(jnp.logical_not(has_previous))
-    def _():
-        fwd[:, 0] = jnp.zeros((4, 8, 8, NZ), jnp.float32)
-
-    @pl.when(jnp.logical_not(has_following))
-    def _():
-        fwd[:, 3] = jnp.zeros((4, 8, 8, NZ), jnp.float32)
-
-    stage_far[:, :, TOP:] = jnp.zeros((2, 2, NY - TOP, NZ), jnp.float32)
-    lane_in = lax.rem(lax.broadcasted_iota(jnp.int32, (3 * NZ, 2 * NZ), 0), NZ)
-    lane_out = lax.broadcasted_iota(jnp.int32, (3 * NZ, 2 * NZ), 1)
-    source_lane = jnp.where(lane_out < NZ, lane_out + 1, lane_out - NZ - 1)
-    shifts[...] = jnp.where(lane_in == source_lane, 1.0, 0.0).astype(jnp.bfloat16)
-
     for copy in own_copies:
         copy.wait()
     for n in range(2):
@@ -213,15 +192,6 @@
         block = both_fields.at[:, pl.ds(at, 2)]
         return [remote(block, block, sib_send.at[i], sib_recv.at[i], pole, sibling)]
 
-    for i in (2, 3, 4, 5, 0, 1):
-        @pl.when(has(steps[i]))
-        def _():
-            for copy in outgoing(i, steps[i]):
-                copy.start()
-
-    for copy in passing(6, own):
-        copy.start()
-
     far_copies = [
         remote(param.at[0], param.at[1], far_send.at[0], far_recv.at[0], partner, space),
         remote(stage.at[pl.ds(2, 2), :, pl.ds(0, TOP)], stage_far.at[:, :, pl.ds(0, TOP)],
@@ -230,8 +200,20 @@
 
     @pl.when(late)
     def _():
-        for copy in far_copies:
-            copy.start()
+        far_copies[0].start()
+
+    for i in (2, 3, 4, 5, 0, 1):
+        @pl.when(has(steps[i]))
+        def _():
+            for copy in outgoing(i, steps[i]):
+                copy.start()
+
+    for copy in passing(6, own):
+        copy.start()
+
+    @pl.when(late)
+    def _():
+        far_copies[1].start()
 
     def to_previous(k):
         return remote(fwd.at[pl.ds(2 * k, 2), 1], fwd.at[pl.ds(2 * k, 2), 3],
@@ -269,6 +251,29 @@
             to_following(k).wait_send()
 
     send_forward(0)
+
+    for step in steps:
+        @pl.when(jnp.logical_not(has(step)))
+        def _():
+            zeros = jnp.zeros((4, 8, 8, NZ), jnp.float32)
+            kap[pl.ds(HALO + 4 * step, 4)] = zeros
+            res[pl.ds(HALO + 4 * step, 4)] = zeros
+
+    @pl.when(jnp.logical_not(has_previous))
+    def _():
+        fwd[:, 0] = jnp.zeros((4, 8, 8, NZ), jnp.float32)
+
+    @pl.when(jnp.logical_not(has_following))
+    def _():
+        fwd[:, 3] = jnp.zeros((4, 8, 8, NZ), jnp.float32)
+
+    stage_far[:, :, TOP:] = jnp.zeros((2, 2, NY - TOP, NZ), jnp.float32)
+    lane_in = lax.broadcasted_iota(jnp.int32, (NZ, NZ), 0)
+    lane_out = lax.broadcasted_iota(jnp.int32, (NZ, NZ), 1)
+    for a, by in enumerate((1, -1)):
+        matrix = jnp.where(lane_in == lane_out + by, 1.0, 0.0).astype(jnp.bfloat16)
+        for k in range(3):
+            shifts[NZ * k : NZ * (k + 1), NZ * a : NZ * (a + 1)] = matrix
 
     block = (8, 8, NZ)
     row = 8 * lax.broadcasted_iota(jnp.int32, block, 1) + lax.broadcasted_iota(jnp.int32, block, 0)
@@ -287,8 +292,12 @@
         fx, bx = k + kap[i + 1], k + kap[i - 1]
         py = k + jnp.where(row_last, 0.0, next_row(k))
         qy = jnp.where(row_first, k, previous_row(py))
-        pz = k + jnp.where(col_last, 0.0, roll(k, -1, 2))
-        qz = jnp.where(col_first, k, roll(pz, 1, 2))
+        if odd:
+            after, before = roll(k, -1, 2), roll(k, 1, 2)
+        else:
+            after, before = lane_sides(k, shifts[...])
+        pz = k + jnp.where(col_last, 0.0, after)
+        qz = k + jnp.where(col_first, 0.0, before)
         my, mz = jnp.where(row_last, 0.0, py), jnp.where(col_last, 0.0, pz)
         face_x[i] = fx
         face_y[i] = my

time: 50.3 us -> 48.4 us (0.962)
  Pallas kernels: 48.3 us -> 46.2 us
    pallas_call x1, Pallas kernels: 48.3 us -> 46.2 us  [per_device(): pl.pallas_call(functools.partial(kernel, chips, poles), out_shape=(pltpu....]
where the time goes in v6:
time: 48.4 us; the launch traced here: 48.1 us
  Pallas kernels  46.2 us (95%)
  local copies, waits for them, and re-layouts  1.26 us (3%)
  between operations  0.64 us (1%)
    pallas_call x1, Pallas kernels, per_device(): pl.pallas_call(functools.partial(kernel, chips, poles), out_shape=(pltpu....  46.2 us
    unnamed x2, local copies, waits for them, and re-layouts  1.26 us

profile of v6, /device:TPU:1, one launch (start us, length us, event | category | flops | bytes accessed | tf_op | source)
XLA Modules:
  0.0 48.1 jit_solution(7966371976945043970)
XLA Ops:
  0.6 46.2 %adjoint_gradient.1 = (f32[2,2,64,128]{3,2,1,0:T(8,128)S(1)}, f32[2,8,128]{2,1,0:T(8,128)S(1)}) custom-call(f32[16]{0:T(128)} %shift_ref.1, f32[16]{0:T(128)} %weight_ref.1, s32[2]{0:T(128)} %order_ref.1, f32[2,64,128]{2,1,0:T(8,128)} %kappa_ref.1, f32[2,64,128]{2,1,0:T(8,128)} %misfit_ref.1, f32[2,2,64,128]{3,2,1,0:T(8,128)} %forward_ref.1), custom_call_target="tpu_custom_call" | custom-call | tf_op jit(solution)/shard_map/adjoint_gradient/pallas_call | solution.py:658
  46.8 0.7 %copy.10 = f32[2,2,64,128]{3,2,1,0:T(8,128)} copy(f32[2,2,64,128]{3,2,1,0:T(8,128)S(1)} %get-tuple-element.2) | data formatting | bytes 262144
  47.5 0.6 %copy.11 = f32[2,8,128]{2,1,0:T(8,128)} copy(f32[2,8,128]{2,1,0:T(8,128)S(1)} %get-tuple-element.3) | data formatting | bytes 16384

commit v7 on v6

--- a/solution.py
+++ b/solution.py
@@ -67,8 +67,8 @@
     shift_ref, weight_ref, order_ref, kappa_ref, misfit_ref, forward_ref,
     adjoint_ref, gradient_ref,
     shift_mem, weight_mem, order_mem,
-    both_fields, face_x, face_y, face_z, down_z, base, diag, gain, z1, z2, rt,
-    cface_x, cface_y, cface_z, cbase, cgain, y1, u0, ut,
+    both_fields, face_x, face_y, face_z, down_z, base, z2, rt,
+    cface_x, cface_y, cface_z, cbase, y1, cgain, diag, gain, z1, u0, ut,
     sib_u, sib_t, fwd, parts, stage, stage_far, term, param, part, sums, swap, pieces, gfar, gnear, shifts,
     loc, near_send, near_recv, sib_send, sib_recv, f_send, f_recv, ar_send, ar_recv, sw_send, sw_recv,
     xs_send, xs_recv, rs_send, rs_recv, far_send, far_recv, y_send, y_recv, token,
@@ -179,7 +179,7 @@
         return [
             remote(block, block, y_send.at[i - 2, d], y_recv.at[i - 2, d],
                    half * half_poles + lax.rem(yy + d, half_poles), space)
-            for d in range(1, half_poles)
+            for d in (half_poles // 2, *(d for d in range(1, half_poles) if d != half_poles // 2))
         ]
 
     def outgoing(i, step):
@@ -307,9 +307,9 @@
         base[i] = b
         d = b + own_shift
         g = jnp.where(inside(i), W, 0.0) / d
-        diag[i] = d
-        gain[i] = g
-        z1[i] = g * res[i]
+        diag[0, i] = d
+        gain[0, i] = g
+        z1[0, i] = g * res[i]
         around = row_pairs(fx if odd else bx), rows_of(qy)[0] + rows_of(py)[1], row_pairs(pz), row_pairs(qz)
         return fx, around, rows_of(my)[1], row_pairs(mz)
 
@@ -324,7 +324,21 @@
         both = (bx0 + bx1) + (by0 + by1)
         d = both + (qz0 + qz1) + roll(both + (pz0 + pz1), -1, 2)
         cbase[j] = d
-        cgain[j] = jnp.where(inside(i), W, 0.0) / (d + 8.0 * own_shift)
+        cgain[0, j] = jnp.where(inside(i), W, 0.0) / (d + 8.0 * own_shift)
+
+    def far_gain(i, shift):
+        d = base[i] + shift
+        g = jnp.where(inside(i), W, 0.0) / d
+        diag[1, i] = d
+        gain[1, i] = g
+        z1[1, i] = g * res[i]
+
+    def far_gains(rows):
+        shift = param[1, 0]
+        for j in rows:
+            far_gain(2 * j, shift)
+            far_gain(2 * j + 1, shift)
+            cgain[1, j] = jnp.where(inside(2 * j), W, 0.0) / (cbase[j] + 8.0 * shift)
 
     middle = HALO // 2
     other = HALO + 2 * (1 - core)
@@ -359,9 +373,20 @@
             rows = (middle - 2 * ring - 1, middle - 2 * ring, middle + 2 * ring + 1, middle + 2 * ring + 2)
         for j in rows:
             faces(j)
+        if ring == 1:
+            @pl.when(early)
+            def _():
+                far_copies[0].wait_recv()
+                far_gains(range(middle - 3, middle + 5))
     face_x[0] = kap[0] + kap[1]
     fine_faces(1, True)
     fine_faces(PLANES - 2, False)
+
+    @pl.when(early)
+    def _():
+        far_gains((*range(1, middle - 3), *range(middle + 5, PLANES // 2 - 1)))
+        far_gain(1, param[1, 0])
+        far_gain(PLANES - 2, param[1, 0])
 
     def off(vm, v, vp, fm, fx, fy):
         total = fx * vp + fm * vm
@@ -389,27 +414,28 @@
 
     fine_xy, coarse_xy = (face_x, face_y), (cface_x, cface_y)
 
-    def precondition(source, out, lo, hi):
+    def precondition(e, source, out, lo, hi):
+        start = z1.at[e]
         first, last = (lo - 1) // 2, hi // 2
         held = []
 
         def down(i, part_off, v):
             held.append(0.2 * source[i] + part_off)
             if i % 2:
-                y1[i // 2] = cgain[i // 2] * pair_sum(held[-2] + held[-1])
+                y1[i // 2] = cgain[e, i // 2] * pair_sum(held[-2] + held[-1])
 
         def up(j, part_off, v):
             i = 2 * j
-            y2 = 1.2 * v + cgain[j] * part_off
+            y2 = 1.2 * v + cgain[e, j] * part_off
             y2 = jnp.where(col_odd, roll(y2, 1, 2), y2)
             y2 = jnp.stack([y2, y2], axis=1).reshape(block)
-            z2[i] = z1[i] + y2
-            z2[i + 1] = z1[i + 1] + y2
+            z2[i] = start[i] + y2
+            z2[i + 1] = start[i + 1] + y2
 
         def smooth(i, part_off, v):
-            out[i] = 0.2 * v + z1[i] + gain[i] * part_off
-
-        sweep(z1, 2 * first - 2, 2 * last + 4, fine_xy, fine_lanes, down)
+            out[i] = 0.2 * v + start[i] + gain[e, i] * part_off
+
+        sweep(start, 2 * first - 2, 2 * last + 4, fine_xy, fine_lanes, down)
         sweep(y1, first, last + 1, coarse_xy, coarse_lanes, up)
         sweep(z2, lo, hi, fine_xy, fine_lanes, smooth)
 
@@ -428,35 +454,22 @@
     part[0] = jnp.zeros((8, NZ), jnp.float32)
 
     def solve(e, carry):
-        @pl.when(e == 1)
-        def _():
-            far_copies[0].wait_recv()
-            shift = param[1, 0]
-            for i in range(1, PLANES - 1):
-                d = base[i] + shift
-                g = jnp.where(inside(i), W, 0.0) / d
-                diag[i] = d
-                gain[i] = g
-                z1[i] = g * res[i]
-            for j in range(1, PLANES // 2 - 1):
-                cgain[j] = jnp.where(inside(2 * j), W, 0.0) / (cbase[j] + 8.0 * shift)
-
         u, t = u0.at[e], ut.at[e]
-        precondition(res, u, HALO - 6, HALO + 10)
+        precondition(e, res, u, HALO - 6, HALO + 10)
 
         def residual(i, part_off, v):
-            value = res[i] - (diag[i] * v - part_off)
+            value = res[i] - (diag[e, i] * v - part_off)
             rt[i] = value
-            z1[i] = gain[i] * value
+            z1[e, i] = gain[e, i] * value
 
         sweep(u, HALO - 5, HALO + 9, fine_xy, fine_lanes, residual)
-        precondition(rt, t, HALO - 1, HALO + 5)
+        precondition(e, rt, t, HALO - 1, HALO + 5)
         for copy in exchange(e):
             copy.start()
         totals = [jnp.zeros((8, NZ), jnp.float32)] * 4
 
         def products(i, part_off, v):
-            image = diag[i] * v - part_off
+            image = diag[e, i] * v - part_off
             un, rn, tn = u[i], res[i], rt[i]
             for k, product in enumerate((un * rn, un * tn, tn * v, v * image)):
                 totals[k] = totals[k] + jnp.sum(product, axis=0)
@@ -666,8 +679,8 @@
             scratch_shapes=[
                 pltpu.SMEM(pole_shifts.shape, f32), pltpu.SMEM(pole_weights.shape, f32),
                 pltpu.SMEM(pole_order.shape, jnp.int32),
-            ] + [pltpu.VMEM((2, PLANES, 8, 8, NZ), f32)] + [fine] * 10 + [coarse] * 6 + [
-                pair, pair, windows, windows, slots, pltpu.VMEM((2, 2, 2, 2, 8, 8, NZ), f32),
+            ] + [pltpu.VMEM((2, PLANES, 8, 8, NZ), f32)] + [fine] * 7 + [coarse] * 5 + [
+                pltpu.VMEM((2, PLANES // 2, 4, 8, NZ), f32), pair, pair, pair, pair, pair, windows, windows, slots, pltpu.VMEM((2, 2, 2, 2, 8, 8, NZ), f32),
                 pltpu.VMEM((4, 2, NY, NZ), f32), pltpu.VMEM((2, 2, NY, NZ), f32),
                 pltpu.VMEM((2, NY, NZ), f32), pltpu.VMEM((2, 2, 8, NZ), f32),
                 pltpu.VMEM((chips, 8, NZ), f32), tile, tile,

time: 48.4 us -> 48.3 us (level)
  no operation moved by 1% of the time
where the time goes in v7:
time: 48.3 us; the launch traced here: 47.9 us
  Pallas kernels  46 us (95%)
  local copies, waits for them, and re-layouts  1.26 us (3%)
  between operations  0.64 us (1%)
    pallas_call x1, Pallas kernels, per_device(): pl.pallas_call(functools.partial(kernel, chips, poles), out_shape=(pltpu....  46 us
    unnamed x2, local copies, waits for them, and re-layouts  1.26 us

profile of v7, /device:TPU:1, one launch (start us, length us, event | category | flops | bytes accessed | tf_op | source)
XLA Modules:
  0.0 47.9 jit_solution(6962571439079769112)
XLA Ops:
  0.6 46.0 %adjoint_gradient.1 = (f32[2,2,64,128]{3,2,1,0:T(8,128)S(1)}, f32[2,8,128]{2,1,0:T(8,128)S(1)}) custom-call(f32[16]{0:T(128)} %shift_ref.1, f32[16]{0:T(128)} %weight_ref.1, s32[2]{0:T(128)} %order_ref.1, f32[2,64,128]{2,1,0:T(8,128)} %kappa_ref.1, f32[2,64,128]{2,1,0:T(8,128)} %misfit_ref.1, f32[2,2,64,128]{3,2,1,0:T(8,128)} %forward_ref.1), custom_call_target="tpu_custom_call" | custom-call | tf_op jit(solution)/shard_map/adjoint_gradient/pallas_call | solution.py:671
  46.6 0.7 %copy.10 = f32[2,2,64,128]{3,2,1,0:T(8,128)} copy(f32[2,2,64,128]{3,2,1,0:T(8,128)S(1)} %get-tuple-element.2) | data formatting | bytes 262144
  47.3 0.6 %copy.11 = f32[2,8,128]{2,1,0:T(8,128)} copy(f32[2,8,128]{2,1,0:T(8,128)S(1)} %get-tuple-element.3) | data formatting | bytes 16384
